TPU v7x, 256 devices: a whole 4x4x8 slice. The times are simulated.
256 devices in a mesh: section: 4 (over x), seq: 32 (over z, y), mp: 2 (over core).
Axes of the slice: x: 4, y: 4, z: 8, core: 2. Of those that a mesh axis runs over, the one named last changes fastest.
Arguments:
- text_embed: bfloat16 [320, 8192], P(None, ('seq', 'mp')), may hold values from -6 to 6
- patch_hidden: bfloat16 [256, 5120], P(('section', 'seq', 'mp')), may hold values from -8 to 8
- merge_weight: bfloat16 [5120, 8192], P(None, ('seq', 'mp')), may hold values from -0.078125 to 0.078125
- merge_bias: bfloat16 [8192], P(('seq', 'mp')), may hold values from -3 to 3
- norm_gain: bfloat16 [4, 8192], P('section'), may hold values from 0.5 to 1.5
- query_weight: bfloat16 [4, 8192, 8192], P('section', None, ('seq', 'mp')), may hold values from -0.62285876 to 0.62285876
- key_weight: bfloat16 [4, 8192, 1024], P('section', None, ('seq', 'mp')), may hold values from -0.62285876 to 0.62285876
- value_weight: bfloat16 [4, 8192, 1024], P('section', None, ('seq', 'mp')), may hold values from -0.055242717 to 0.055242717
- image_counts: int32 [2, 4], replicated, may hold values from 1 to 64, 128 in all within a row
- text_counts: int32 [2, 4], replicated, may hold values from 1 to 16, 32 in all within a row
Outputs:
- hidden_states: bfloat16 [4, 320, 8192], P('section', None, ('seq', 'mp'))
Inputs may be any that keep to these rules, and one draw needn't show every extreme that they name: `image_counts`: each micro-batch's image counts sum to 256 / 2. `text_counts`: each micro-batch's image and text counts together sum to 160.
All inputs are finite; a program needn't handle non-finite values.
Results may differ from a plain program's by a relative error of at most 0.017.
Values may be sent and summed in bfloat16 or wider, within the bound.
A program may use at most 64 MiB of HBM per device.

v0:
```python
import math

import jax
import jax.numpy as jnp
from jax import lax
from jax.sharding import PartitionSpec as P

HEADS = 64
HD = 128
KV_HEADS = 8


def from_behind(block, axis, distance):
    devices = range(lax.axis_size(axis))
    route = [(i - distance, i) for i in devices if i - distance in devices]
    return lax.ppermute(block, axis, route)


def layout(image_counts, text_counts, tokens):
    lengths = (image_counts + text_counts).reshape(-1)
    images = image_counts.reshape(-1)
    ends = jnp.cumsum(lengths)
    starts = ends - lengths
    before = jnp.cumsum(images) - images
    position = jnp.arange(tokens, dtype=jnp.int32)
    request = jnp.sum((position[:, None] >= ends[None, :]).astype(jnp.int32), axis=1)
    member = request[:, None] == jnp.arange(lengths.shape[0], dtype=jnp.int32)[None, :]
    first = jnp.sum(jnp.where(member, starts[None, :], 0), axis=1)
    count = jnp.sum(jnp.where(member, images[None, :], 0), axis=1)
    earlier = jnp.sum(jnp.where(member, before[None, :], 0), axis=1)
    offset = position - first
    is_image = (offset >= 1) & (offset <= count)
    row_index = jnp.where(is_image, earlier + offset - 1, 0)
    return (request, is_image, row_index)


def pick_groups(gathered, first_group, local_groups):
    rows_here = gathered.shape[0]
    shaped = gathered.reshape(rows_here, HD, KV_HEADS)
    picked = lax.dynamic_slice_in_dim(shaped, first_group, local_groups, 2)
    return jnp.swapaxes(picked, 1, 2).reshape(rows_here, local_groups * HD)


def shards(
    text_embed,
    patch_hidden,
    merge_weight,
    merge_bias,
    norm_gain,
    query_weight,
    key_weight,
    value_weight,
    image_counts,
    text_counts,
):
    tokens, columns = text_embed.shape
    heads_here = columns // HD
    group_size = HEADS // KV_HEADS
    local_groups = max(1, heads_here // group_size)
    shared_heads = heads_here // local_groups
    first_group = lax.axis_index(("seq", "mp")) * heads_here // group_size
    bias_f = merge_bias.astype(jnp.float32)
    act = jax.nn.gelu(
        lax.all_gather(patch_hidden, ("seq", "mp"), axis=0, tiled=True).astype(jnp.float32),
        approximate=False,
    ).astype(jnp.bfloat16)
    section_rows = (jnp.dot(act, merge_weight, preferred_element_type=jnp.float32) + bias_f).astype(
        jnp.bfloat16
    )
    merged = lax.all_gather(section_rows, "section", axis=0, tiled=True)
    request, is_image, row_index = layout(image_counts, text_counts, tokens)
    start_state = jnp.where(is_image[:, None], jnp.take(merged, row_index, axis=0), text_embed)
    blocks = 2
    rows = tokens // blocks
    depth = lax.axis_size("section")
    section_here = lax.axis_index("section")
    gain = norm_gain[0].astype(jnp.float32)[None, :]
    position = jnp.arange(tokens, dtype=jnp.int32)
    key_cache = jnp.zeros((tokens, local_groups * HD), jnp.bfloat16)
    value_cache = jnp.zeros((tokens, local_groups * HD), jnp.bfloat16)
    hidden = jnp.zeros((tokens, columns), jnp.bfloat16)
    incoming = jnp.zeros((rows, columns), jnp.bfloat16)
    turns = blocks + depth - 1
    for tick in range(turns):
        block = tick - section_here
        valid = (block >= 0) & (block < blocks)
        first_row = jnp.clip(block, 0, blocks - 1) * rows
        if tick < blocks:
            fresh = start_state[tick * rows : (tick + 1) * rows]
            current = jnp.where(section_here == 0, fresh, incoming)
        else:
            current = incoming
        whole = lax.all_gather(current, ("seq", "mp"), axis=1, tiled=True)
        xf = whole.astype(jnp.float32)
        scale = lax.rsqrt(jnp.mean(xf * xf, axis=1, keepdims=True) + 1e-06)
        normed = (xf * scale * gain).astype(jnp.bfloat16)
        query = jnp.dot(normed, query_weight[0], preferred_element_type=jnp.float32).astype(
            jnp.bfloat16
        )
        key_part = jnp.dot(normed, key_weight[0], preferred_element_type=jnp.float32).astype(
            jnp.bfloat16
        )
        value_part = jnp.dot(normed, value_weight[0], preferred_element_type=jnp.float32).astype(
            jnp.bfloat16
        )
        key_all, value_all = (
            lax.all_gather(key_part, ("seq", "mp"), axis=1, tiled=True),
            lax.all_gather(value_part, ("seq", "mp"), axis=1, tiled=True),
        )
        key = pick_groups(key_all, first_group, local_groups)
        value = pick_groups(value_all, first_group, local_groups)
        key_cache = jnp.where(
            valid, lax.dynamic_update_slice_in_dim(key_cache, key, first_row, 0), key_cache
        )
        value_cache = jnp.where(
            valid, lax.dynamic_update_slice_in_dim(value_cache, value, first_row, 0), value_cache
        )
        query_request = lax.dynamic_slice_in_dim(request, first_row, rows)
        query_position = first_row + jnp.arange(rows, dtype=jnp.int32)
        allowed = (request[None, :] == query_request[:, None]) & (
            position[None, :] <= query_position[:, None]
        )
        scores = jnp.einsum(
            "qngd,knd->ngqk",
            query.reshape(rows, local_groups, shared_heads, HD),
            key_cache.reshape(tokens, local_groups, HD),
            preferred_element_type=jnp.float32,
        ) / math.sqrt(HD)
        scores = jnp.where(allowed[None, None, :, :], scores, -1e30)
        probs = jax.nn.softmax(scores, axis=-1).astype(jnp.bfloat16)
        attended = jnp.einsum(
            "ngqk,knd->qngd",
            probs,
            value_cache.reshape(tokens, local_groups, HD),
            preferred_element_type=jnp.float32,
        ).reshape(rows, columns)
        state = (current.astype(jnp.float32) + attended).astype(jnp.bfloat16)
        hidden = jnp.where(
            valid, lax.dynamic_update_slice_in_dim(hidden, state, first_row, 0), hidden
        )
        if tick + 1 < turns:
            incoming = from_behind(state, "section", 1)
    return hidden[None]


def solution(mesh):
    in_specs = (
        P(None, ("seq", "mp")),
        P(("section", "seq", "mp"), None),
        P(None, ("seq", "mp")),
        P(("seq", "mp")),
        P("section", None),
        P("section", None, ("seq", "mp")),
        P("section", None, ("seq", "mp")),
        P("section", None, ("seq", "mp")),
        P(),
        P(),
    )
    out_specs = P("section", None, ("seq", "mp"))
    return jax.shard_map(shards, mesh=mesh, in_specs=in_specs, out_specs=out_specs, check_vma=False)
```

profile of v0, /device:TPU:39, one launch (start us, length us, event | category | flops | bytes accessed | tf_op | source)
XLA Modules:
  0.0 1015.3 jit_solution(12970196134366100098)
XLA Ops:
  9.1 53.6 %all-gather = bf16[64,1,5120]{2,1,0:T(2,128)(2,1)S(1)} all-gather(bf16[1,1,5120]{2,1,0:T(2,128)(2,1)} %bitcast.312), channel_id=1, replica_groups=mesh['section'=4,'seq'=32,'mp'=2] {'seq','mp'}, dimensions={0}, use_global_device_ids=true | all-gather | bytes 665600 | tf_op jit(solution)/shard_map/all_gather | solution.py:64
  67.1 4.7 fusion.80
  71.8 9.0 all_gather.52
  83.2 73.4 %all-gather.7.cloned.1.call-done = bf16[160,8192]{1,0:T(8,128)(2,1)} async-done(((bf16[160,128]{1,0:T(8,128)(2,1)}), bf16[160,8192]{1,0:T(8,128)(2,1)}) %all-gather.7.cloned.1.call-update) | async-done | bytes 2621456 | tf_op jit(solution)/shard_map/all_gather | solution.py:93
  162.2 50.2 %all_gather.55 = bf16[160,1024]{0,1:T(8,128)(2,1)S(1)} all-gather(bf16[160,16]{0,1:T(8,128)(2,1)S(1)} %convolution_convert_fusion.8), channel_id=1, replica_groups=mesh['section'=4,'seq'=32,'mp'=2] {'seq','mp'}, dimensions={1}, use_global_device_ids=true | all-gather | bytes 332800 | tf_op jit(solution)/shard_map/all_gather | solution.py:107
  215.2 47.9 %all_gather.54 = bf16[160,1024]{0,1:T(8,128)(2,1)S(1)} all-gather(bf16[160,16]{0,1:T(8,128)(2,1)S(1)} %convolution_convert_fusion.9), channel_id=1, replica_groups=mesh['section'=4,'seq'=32,'mp'=2] {'seq','mp'}, dimensions={1}, use_global_device_ids=true | all-gather | bytes 332800 | tf_op jit(solution)/shard_map/all_gather | solution.py:108
  263.4 2.8 fusion.149
  268.1 3.4 collective-permute-done
  272.3 72.8 %all-gather.9.cloned.1.call-done = bf16[160,8192]{1,0:T(8,128)(2,1)} async-done(((bf16[160,128]{1,0:T(8,128)(2,1)}), bf16[160,8192]{1,0:T(8,128)(2,1)}) %all-gather.9.cloned.1.call-update) | async-done | bytes 2621456 | tf_op jit(solution)/shard_map/all_gather | solution.py:93
  350.0 50.4 %all_gather.57 = bf16[160,1024]{0,1:T(8,128)(2,1)S(1)} all-gather(bf16[160,16]{0,1:T(8,128)(2,1)S(1)} %convolution_convert_fusion.7), channel_id=1, replica_groups=mesh['section'=4,'seq'=32,'mp'=2] {'seq','mp'}, dimensions={1}, use_global_device_ids=true | all-gather | bytes 332800 | tf_op jit(solution)/shard_map/all_gather | solution.py:108
  400.6 47.9 %all_gather.58 = bf16[160,1024]{0,1:T(8,128)(2,1)S(1)} all-gather(bf16[160,16]{0,1:T(8,128)(2,1)S(1)} %convolution_convert_fusion.6), channel_id=1, replica_groups=mesh['section'=4,'seq'=32,'mp'=2] {'seq','mp'}, dimensions={1}, use_global_device_ids=true | all-gather | bytes 332800 | tf_op jit(solution)/shard_map/all_gather | solution.py:107
  453.5 3.4 collective-permute-done.1
  457.7 72.8 %all-gather.11.cloned.1.call-done = bf16[160,8192]{1,0:T(8,128)(2,1)} async-done(((bf16[160,128]{1,0:T(8,128)(2,1)}), bf16[160,8192]{1,0:T(8,128)(2,1)}) %all-gather.11.cloned.1.call-update) | async-done | bytes 2621456 | tf_op jit(solution)/shard_map/all_gather | solution.py:93
  535.3 50.1 %all_gather.61 = bf16[160,1024]{0,1:T(8,128)(2,1)S(1)} all-gather(bf16[160,16]{0,1:T(8,128)(2,1)S(1)} %convolution_convert_fusion.4), channel_id=1, replica_groups=mesh['section'=4,'seq'=32,'mp'=2] {'seq','mp'}, dimensions={1}, use_global_device_ids=true | all-gather | bytes 332800 | tf_op jit(solution)/shard_map/all_gather | solution.py:107
  585.7 47.9 %all_gather.60 = bf16[160,1024]{0,1:T(8,128)(2,1)S(1)} all-gather(bf16[160,16]{0,1:T(8,128)(2,1)S(1)} %convolution_convert_fusion.5), channel_id=1, replica_groups=mesh['section'=4,'seq'=32,'mp'=2] {'seq','mp'}, dimensions={1}, use_global_device_ids=true | all-gather | bytes 332800 | tf_op jit(solution)/shard_map/all_gather | solution.py:108
  638.6 3.4 collective-permute-done.2
  642.8 72.8 %all-gather.13.cloned.1.call-done = bf16[160,8192]{1,0:T(8,128)(2,1)} async-done(((bf16[160,128]{1,0:T(8,128)(2,1)}), bf16[160,8192]{1,0:T(8,128)(2,1)}) %all-gather.13.cloned.1.call-update) | async-done | bytes 2621456 | tf_op jit(solution)/shard_map/all_gather | solution.py:93
  720.5 50.2 %all_gather.64 = bf16[160,1024]{0,1:T(8,128)(2,1)S(1)} all-gather(bf16[160,16]{0,1:T(8,128)(2,1)S(1)} %convolution_convert_fusion.2), channel_id=1, replica_groups=mesh['section'=4,'seq'=32,'mp'=2] {'seq','mp'}, dimensions={1}, use_global_device_ids=true | all-gather | bytes 332800 | tf_op jit(solution)/shard_map/all_gather | solution.py:107
  770.9 47.9 %all_gather.63 = bf16[160,1024]{0,1:T(8,128)(2,1)S(1)} all-gather(bf16[160,16]{0,1:T(8,128)(2,1)S(1)} %convolution_convert_fusion.3), channel_id=1, replica_groups=mesh['section'=4,'seq'=32,'mp'=2] {'seq','mp'}, dimensions={1}, use_global_device_ids=true | all-gather | bytes 332800 | tf_op jit(solution)/shard_map/all_gather | solution.py:108
  823.8 3.4 collective-permute-done.3
  828.6 72.2 %all-gather.15.cloned.1.call-done = bf16[160,8192]{1,0:T(8,128)(2,1)} async-done(((bf16[160,128]{1,0:T(8,128)(2,1)}), bf16[160,8192]{1,0:T(8,128)(2,1)}) %all-gather.15.cloned.1.call-update) | async-done | bytes 2621456 | tf_op jit(solution)/shard_map/all_gather | solution.py:93
  905.6 50.0 %all_gather.67 = bf16[160,1024]{0,1:T(8,128)(2,1)S(1)} all-gather(bf16[160,16]{0,1:T(8,128)(2,1)S(1)} %convolution_convert_fusion), channel_id=1, replica_groups=mesh['section'=4,'seq'=32,'mp'=2] {'seq','mp'}, dimensions={1}, use_global_device_ids=true | all-gather | bytes 332800 | tf_op jit(solution)/shard_map/all_gather | solution.py:107
  955.9 48.2 %all_gather.66 = bf16[160,1024]{0,1:T(8,128)(2,1)S(1)} all-gather(bf16[160,16]{0,1:T(8,128)(2,1)S(1)} %convolution_convert_fusion.1), channel_id=1, replica_groups=mesh['section'=4,'seq'=32,'mp'=2] {'seq','mp'}, dimensions={1}, use_global_device_ids=true | all-gather | bytes 332800 | tf_op jit(solution)/shard_map/all_gather | solution.py:108
  1004.4 2.8 fusion.161
  (161 shorter events, 59.6 us)
Async XLA Ops:
  6.5 256.9 %copy-start = (bf16[1,8192,128]{2,1,0:T(8,128)(2,1)S(1)}, bf16[1,8192,128]{2,1,0:T(8,128)(2,1)}, u32[]{:S(2)}) copy-start(bf16[1,8192,128]{2,1,0:T(8,128)(2,1)} %param.15) | copy-start | bytes 6291460
  6.5 150.1 %all-gather.7.cloned.1.call-start = ((), (), s32[]{:S(2)}) async-start(), calls=%async_computation | async-start | bytes 2662400 | tf_op jit(solution)/shard_map/all_gather | solution.py:93
  62.6 4.4 copy-start.23
  67.0 15.1 %copy-start.15 = (bf16[320,128]{1,0:T(8,128)(2,1)S(1)}, bf16[320,128]{1,0:T(8,128)(2,1)}, u32[]{:S(2)}) copy-start(bf16[320,128]{1,0:T(8,128)(2,1)} %param.10) | copy-start | bytes 245764
  67.1 16.0 %copy-start.22 = (bf16[1,8192]{1,0:T(2,128)(2,1)S(1)}, bf16[1,8192]{1,0:T(2,128)(2,1)}, u32[]{:S(2)}) copy-start(bf16[1,8192]{1,0:T(2,128)(2,1)} %param.14) | copy-start | bytes 49156
  83.0 262.1 %all-gather.9.cloned.1.call-start = ((), (), s32[]{:S(2)}) async-start(), calls=%async_computation.1 | async-start | bytes 2662400 | tf_op jit(solution)/shard_map/all_gather | solution.py:93
  156.6 2.5 copy-start.6
  161.4 51.2 %copy-start.12 = (bf16[1,8192,16]{1,2,0:T(8,128)(2,1)S(1)}, bf16[1,8192,16]{1,2,0:T(8,128)(2,1)}, u32[]{:S(2)}) copy-start(bf16[1,8192,16]{1,2,0:T(8,128)(2,1)} %param.17) | copy-start | bytes 786436
  263.4 3.1 copy-start.13
  266.8 4.7 collective-permute-start
  272.2 258.3 %all-gather.11.cloned.1.call-start = ((), (), s32[]{:S(2)}) async-start(), calls=%async_computation.2 | async-start | bytes 2662400 | tf_op jit(solution)/shard_map/all_gather | solution.py:93
  345.1 2.5 copy-start.8
  448.9 3.1 copy-start.14
  452.2 4.7 collective-permute-start.1
  457.6 258.1 %all-gather.13.cloned.1.call-start = ((), (), s32[]{:S(2)}) async-start(), calls=%async_computation.3 | async-start | bytes 2662400 | tf_op jit(solution)/shard_map/all_gather | solution.py:93
  530.5 2.5 copy-start.9
  634.0 3.1 copy-start.19
  637.3 4.7 collective-permute-start.2
  642.7 258.1 %all-gather.15.cloned.1.call-start = ((), (), s32[]{:S(2)}) async-start(), calls=%async_computation.4 | async-start | bytes 2662400 | tf_op jit(solution)/shard_map/all_gather | solution.py:93
  715.6 2.5 copy-start.10
  819.2 3.1 copy-start.21
  822.5 4.7 collective-permute-start.3
  900.8 2.5 copy-start.7
  1004.4 3.1 copy-start.17
  (9 other events, 11.9 us)
Sparse Core Ops, SparseCore 0:
  83.1 73.4 all-gather.6
  272.3 72.7 all-gather.8
  457.7 72.7 all-gather.10
  642.9 72.7 all-gather.12
  828.0 72.7 all-gather.14
where the time goes:
time: 1030 us; the launch traced here: 1020 us
  blocking collectives  553 us (54%)
  waiting for transfers between devices  378 us (37%)
  matrix products  30.4 us (3%)
  other arithmetic  24.1 us (2%)
  between operations  14.2 us (1%)
    all_gather x5, waiting for transfers between devices, shards(): whole = lax.all_gather(current, ('seq', 'mp'), axis=1, tiled=True)  364 us
    all_gather x5, blocking collectives, shards(): lax.all_gather(key_part, ('seq', 'mp'), axis=1, tiled=True)  248 us
    all_gather x5, blocking collectives, shards(): lax.all_gather(value_part, ('seq', 'mp'), axis=1, tiled=True)  242 us
    all_gather x1, blocking collectives, shards(): lax.all_gather(patch_hidden, ('seq', 'mp'), axis=0, tiled=True)  53.6 us
  transfers between devices with their start and end apart: 9, of which 9 were waited for; matrix products, arithmetic and copies ran while one was open for 0% of the time, Pallas kernels for 0%

commit v1 on v0

v1 whole, which is shorter than its diff:
```python
import functools
import math

import jax
import jax.numpy as jnp
from jax import lax
from jax.experimental import pallas as pl
from jax.experimental.pallas import tpu as pltpu
from jax.sharding import PartitionSpec as P

MESH = pl.DeviceIdType.MESH
F32 = jnp.float32
BF16 = jnp.bfloat16
HD = 128
NY = 4
NZ = 8
CHUNKS = 4
Z_ORDER = (4, 3, 5, 2, 6, 1, 7)


def iota(shape, dim):
    return lax.broadcasted_iota(jnp.int32, shape, dim)


def dot(a, b):
    return lax.dot_general(a, b, (((1,), (0,)), ((), ())), preferred_element_type=F32)


def dot_t(a, b):
    return lax.dot_general(a, b, (((1,), (1,)), ((), ())), preferred_element_type=F32)


def drain(ref, sem):
    pltpu.make_async_copy(ref, ref, sem).wait()


def kernel(
    images_ref,
    texts_ref,
    text_ref,
    patch_ref,
    mw_ref,
    bias_ref,
    gain_ref,
    wq_ref,
    wk_ref,
    wv_ref,
    out_ref,
    gains,
    actf,
    act,
    rows,
    rowsf,
    part,
    merged,
    start,
    kvtx,
    kvrx,
    kvrows,
    kvmine,
    wq_sib,
    weights,
    states,
    xs,
    xr,
    kvx,
    spread,
    keys,
    values,
    s_act,
    r_act1,
    r_act2,
    r_act3,
    s_wq,
    r_wq,
    s_kv,
    r_kv,
    s_kvm,
    r_kvm,
    s_part,
    r_part,
    s_init,
    s_st,
    r_st,
    s_fw,
    r_fw,
    s_x,
    r_x,
    s_kx,
    r_kx,
):
    sec = lax.axis_index("section")
    seq = lax.axis_index("seq")
    core = lax.axis_index("mp")
    depth = lax.axis_size("section")
    z = seq // NY
    y = seq % NY
    tokens = out_ref.shape[0]
    tc = tokens // CHUNKS
    batch = tokens // images_ref.shape[0]
    per_batch = batch // tc

    def at_z(dz, s=None):
        return (sec if s is None else s, ((z + dz) % NZ) * NY + y, core)

    def at_y(dy):
        return (sec, z * NY + (y + dy) % NY, core)

    sibling = (sec, seq, 1 - core)

    def send(src, dst, ssem, rsem, device):
        pltpu.make_async_remote_copy(
            src_ref=src, dst_ref=dst, send_sem=ssem, recv_sem=rsem, device_id=device, device_id_type=MESH
        ).start()

    barrier = pltpu.get_barrier_semaphore()

    def greet(device):
        pl.semaphore_signal(barrier, inc=1, device_id=device, device_id_type=MESH)

    for dz in Z_ORDER:
        greet(at_z(dz))
    for dy in (2, 1, 3):
        greet(at_y(dy))
    greet(sibling)

    @pl.when(sec > 0)
    def _():
        for dz in (0,) + Z_ORDER:
            greet(at_z(dz, sec - 1))

    @pl.when(sec == 0)
    def _():
        for other in (1, 2, 3):
            greet((other, seq, core))

    for k in range(40):
        actf[k : k + 1, :] = patch_ref[:, k * 128 : (k + 1) * 128].astype(F32)
    xa = actf[...]
    act[...] = (0.5 * xa * (1.0 + lax.erf(xa * math.sqrt(0.5)))).astype(BF16)
    for k in range(64):
        gains[k : k + 1, :] = gain_ref[:, k * 128 : (k + 1) * 128].astype(F32)

    r_i, c_i = iota((128, 128), 0), iota((128, 128), 1)
    deal = (
        ((r_i >> 4) == (c_i & 7)) & (((r_i >> 2) & 3) == (c_i >> 5)) & ((r_i & 3) == ((c_i >> 3) & 3))
    )
    deal = jnp.where(deal, 1.0, 0.0).astype(BF16)
    for t in range(16):
        pieces = []
        for b in range(4):
            lanes = slice((4 * t + b) * 128, (4 * t + b + 1) * 128)
            pieces += [wk_ref[:, lanes], wv_ref[:, lanes]]
        kvtx[:, t] = dot(deal, jnp.concatenate(pieces, axis=0)).astype(BF16).reshape(NZ, 16, 128)
    for q in range(32):
        kvmine[q // NY, q % NY, 2] = jnp.zeros((32, 128), BF16)
        kvmine[q // NY, q % NY, 3] = jnp.zeros((32, 128), BF16)
    r_i, c_i = iota((512, 256), 0), iota((512, 256), 1)
    lane = r_i & 127
    feature = 2 * ((lane & 7) * 8 + (r_i >> 7) * 2 + ((lane >> 5) & 1)) + ((lane >> 3) & 1)
    natural = (lane < 64) & (c_i == ((lane >> 4) & 1) * 128 + feature)
    spread[...] = jnp.where(natural, 1.0, 0.0).astype(BF16)

    @pl.when(sec == 0)
    def _():
        pl.semaphore_wait(barrier, 19)

    @pl.when((sec > 0) & (sec < depth - 1))
    def _():
        pl.semaphore_wait(barrier, 20)

    @pl.when(sec == depth - 1)
    def _():
        pl.semaphore_wait(barrier, 12)

    for dz in Z_ORDER:
        send(act, rows.at[core, z, y], s_act.at[0], r_act1, at_z(dz))
    pltpu.make_async_copy(act, rows.at[core, z, y], r_act1).start()
    send(wq_ref.at[:, :, 1 - core], wq_sib, s_wq, r_wq, sibling)

    def scaled(q, w):
        g = gains[pl.ds(2 * q + core, 1), :]
        d = jnp.where(iota((128, 128), 0) == iota((128, 128), 1), g, 0.0).astype(BF16)
        return d, dot(d, w).astype(BF16)

    @pl.loop(0, 32)
    def _(q):
        zz, yy = q // NY, q % NY
        weights[zz, yy, :, 0:128] = scaled(q, wq_ref[zz, yy, core])[1]

    drain(rows.at[core, :, 0], r_act1)
    for i, dy in enumerate((2, 1, 3)):
        send(rows.at[core, :, y], rows.at[core, :, y], s_act.at[1], r_act2, at_y(dy))
    for dz in Z_ORDER:
        send(kvtx.at[(z + dz) % NZ], kvrx.at[z], s_kv, r_kv, at_z(dz))
    pltpu.make_async_copy(kvtx.at[z], kvrx.at[z], r_kv).start()

    drain(wq_sib, r_wq)

    @pl.loop(0, 32)
    def _(q):
        zz, yy = q // NY, q % NY
        weights[zz, yy, :, 128:256] = scaled(q, wq_sib[zz, yy])[1]

    drain(rows.at[core, :, pl.ds(0, 3)], r_act2)
    send(rows.at[core], rows.at[core], s_act.at[2], r_act3, sibling)
    drain(rows.at[core], r_act3)

    for p in range(2):
        for zz in range(NZ):
            for yy in range(NY):
                at = ((p * NZ + zz) * NY + yy) * 40
                rowsf[at : at + 40, :] = rows[p, zz, yy].astype(F32)
    acc = jnp.broadcast_to(bias_ref[...].astype(F32), (64, 128))
    for k in range(20):
        xk = jnp.concatenate(
            [rowsf[pl.ds(2 * k, 64, stride=40), :], rowsf[pl.ds(2 * k + 1, 64, stride=40), :]], axis=1
        ).astype(BF16)
        acc = acc + dot(xk, mw_ref[256 * k : 256 * (k + 1), :])
    part[...] = acc.astype(BF16)

    @pl.when(sec > 0)
    def _():
        send(part, merged.at[sec], s_part, r_part, (0, seq, core))

    def place(rows_here, first):
        pos = first + iota((rows_here, 1), 0)
        begin = jnp.zeros((rows_here, 1), jnp.int32)
        count = jnp.zeros((rows_here, 1), jnp.int32)
        earlier = jnp.zeros((rows_here, 1), jnp.int32)
        at, seen = jnp.int32(0), jnp.int32(0)
        for b in range(images_ref.shape[0]):
            for r in range(images_ref.shape[1]):
                image, text = images_ref[b, r], texts_ref[b, r]
                inside = pos >= at
                begin = jnp.where(inside, at, begin)
                count = jnp.where(inside, image, count)
                earlier = jnp.where(inside, seen, earlier)
                at, seen = at + image + text, seen + image
        return pos, begin, count, earlier

    @pl.when(sec == 0)
    def _():
        merged[0] = part[...]
        pos, begin, count, earlier = place(tokens, 0)
        offset = pos - begin
        is_image = (offset >= 1) & (offset <= count)
        row = earlier + offset - 1
        slot = (row & ~63) + ((row & 1) << 5) + ((row & 63) >> 1)
        chosen = (iota((tokens, 256), 1) == slot) & is_image
        drain(merged.at[pl.ds(1, 3)], r_part)
        picked = dot(jnp.where(chosen, 1.0, 0.0).astype(BF16), merged[...].reshape(256, 128))
        start[...] = jnp.where(is_image, picked, text_ref[...].astype(F32)).astype(BF16)
        for t in range(CHUNKS):
            src = start.at[pl.ds(t * tc, tc)]
            for dz in Z_ORDER:
                send(src, states.at[t, z, y], s_init.at[t], r_st.at[t], at_z(dz))
            pltpu.make_async_copy(src, states.at[t, z, y], r_st.at[t]).start()

    drain(kvrx, r_kv)
    r_i, c_i = iota((128, 128), 0), iota((128, 128), 1)
    collect = ((r_i >> 5) == ((c_i >> 2) & 3)) & (((r_i >> 3) & 3) == (c_i & 3)) & ((r_i & 7) == (c_i >> 4))
    collect = jnp.where(collect, 1.0, 0.0).astype(BF16)
    for t in range(16):
        made = dot(collect, kvrx[:, t].reshape(128, 128)).astype(BF16).reshape(2, 2, 32, 128)
        for h in range(2):
            kvrows[t // 2, (t % 2) * 2 + h] = made[h]
    send(kvrows.at[:, :, 1 - core], kvmine.at[:, :, core], s_kvm, r_kvm, sibling)
    mine = pltpu.make_async_copy(kvrows.at[:, :, core], kvmine.at[:, :, core], s_kvm)
    mine.start()

    def forward(t):
        drain(states.at[t, :, 0], r_st.at[t])
        for dy in (2, 1, 3):
            send(states.at[t, :, y], states.at[t, :, y], s_fw.at[t], r_fw.at[t], at_y(dy))

    forward(0)
    drain(kvmine.at[:, :, 0], r_kvm)
    drain(kvmine.at[:, :, pl.ds(0, 2)], s_kvm)

    @pl.loop(0, 32)
    def _(q):
        zz, yy = q // NY, q % NY
        g = gains[pl.ds(2 * q + core, 1), :]
        d = jnp.where(iota((128, 128), 0) == iota((128, 128), 1), g, 0.0).astype(BF16)
        weights[zz, yy, :, 256:384] = dot_t(d, kvmine[zz, yy].reshape(128, 128)).astype(BF16)

    for t in range(CHUNKS):
        if t + 1 < CHUNKS:
            forward(t + 1)
        drain(states.at[t, :, pl.ds(0, 3)], r_fw.at[t])

        def products(zz, carry):
            acc, squares = carry
            x = jnp.concatenate([states[t, zz, yy] for yy in range(NY)], axis=1)
            acc = acc + dot(x, weights[zz].reshape(NY * 128, 384))
            xf = x.astype(F32)
            for yy in range(NY):
                piece = xf[:, yy * 128 : (yy + 1) * 128]
                squares = squares + piece * piece
            return acc, squares

        acc, squares = lax.fori_loop(
            0, NZ, products, (jnp.zeros((tc, 384), F32), jnp.zeros((tc, 128), F32)), unroll=2
        )
        total = jnp.sum(squares, axis=1, keepdims=True)
        low = iota((tc, 128), 1) < 64
        mixed = jnp.where(low, acc[:, 256:384], total)
        xs[t, :, 0:128] = acc[:, 128:256]
        xs[t, :, 128:256] = mixed
        send(xs.at[t], xr.at[t], s_x.at[t], r_x.at[t], sibling)
        own = acc[:, 0:128]
        pos, begin, _, _ = place(tc, t * tc)
        drain(xr.at[t], r_x.at[t])
        mixed = mixed + xr[t, :, 128:256]
        scale = lax.rsqrt(mixed[:, 64:65] * (1.0 / 8192.0) + 1e-6)
        kvx[t, y] = jnp.where(low, mixed * scale, 0.0).astype(BF16)
        for dy in (2, 1, 3):
            send(kvx.at[t, y], kvx.at[t, y], s_kx.at[t], r_kx.at[t], at_y(dy))
        query = ((own + xr[t, :, 0:128]) * scale).astype(BF16)
        first = (t // per_batch) * batch
        span = (t % per_batch + 1) * tc
        column = first + iota((tc, span), 1)
        allowed = (column >= begin) & (column <= pos)
        drain(kvx.at[t, pl.ds(0, 3)], r_kx.at[t])
        kv = dot(jnp.concatenate([kvx[t, yy] for yy in range(NY)], axis=1), spread[...]).astype(BF16)
        keys[t * tc : (t + 1) * tc, :] = kv[:, 0:128]
        values[t * tc : (t + 1) * tc, :] = kv[:, 128:256]
        scores = dot_t(query, keys[first : first + span, :]) * (1.0 / math.sqrt(HD))
        scores = jnp.where(allowed, scores, -1e30)
        weight = jnp.exp(scores - jnp.max(scores, axis=1, keepdims=True))
        probs = (weight / jnp.sum(weight, axis=1, keepdims=True)).astype(BF16)
        attended = dot(probs, values[first : first + span, :])
        state = states[t, z, y].astype(F32) + attended
        out_ref[t * tc : (t + 1) * tc, :] = state.astype(BF16)

        @pl.when(sec < depth - 1)
        def _():
            for dz in Z_ORDER + (0,):
                send(
                    out_ref.at[pl.ds(t * tc, tc)], states.at[t, z, y], s_st.at[t], r_st.at[t], at_z(dz, sec + 1)
                )

    drain(rows.at[core, pl.ds(0, 7), 0], s_act.at[0])
    drain(rows.at[core, :, pl.ds(0, 3)], s_act.at[1])
    drain(rows.at[core], s_act.at[2])
    drain(wq_sib, s_wq)
    drain(kvrx.at[pl.ds(0, 7)], s_kv)

    @pl.when(sec > 0)
    def _():
        drain(part, s_part)

    for t in range(CHUNKS):

        @pl.when(sec == 0)
        def _():
            drain(states.at[t, pl.ds(0, 7), 0], s_init.at[t])

        @pl.when(sec < depth - 1)
        def _():
            drain(states.at[t, :, 0], s_st.at[t])

        drain(states.at[t, :, pl.ds(0, 3)], s_fw.at[t])
        drain(xs.at[t], s_x.at[t])
        drain(kvx.at[t, pl.ds(0, 3)], s_kx.at[t])


def shards(text_embed, patch, mw, bias, gain, wq, wk, wv, images, texts):
    tokens = text_embed.shape[0]
    tc = tokens // CHUNKS
    vmem = pl.BlockSpec(memory_space=pltpu.VMEM)
    smem = pl.BlockSpec(memory_space=pltpu.SMEM)
    dma = pltpu.SemaphoreType.DMA
    scratch = [
        pltpu.VMEM((64, 128), F32),
        pltpu.VMEM((40, 128), F32),
        pltpu.VMEM((40, 128), BF16),
        pltpu.VMEM((2, NZ, NY, 40, 128), BF16),
        pltpu.VMEM((2560, 128), F32),
        pltpu.VMEM((64, 128), BF16),
        pltpu.VMEM((4, 64, 128), BF16),
        pltpu.VMEM((tokens, 128), BF16),
        pltpu.VMEM((NZ, 16, 16, 128), BF16),
        pltpu.VMEM((NZ, 16, 16, 128), BF16),
        pltpu.VMEM((NZ, NY, 2, 32, 128), BF16),
        pltpu.VMEM((NZ, NY, 4, 32, 128), BF16),
        pltpu.VMEM((NZ, NY, 128, 128), BF16),
        pltpu.VMEM((NZ, NY, 128, 384), BF16),
        pltpu.VMEM((CHUNKS, NZ, NY, tc, 128), BF16),
        pltpu.VMEM((CHUNKS, tc, 256), F32),
        pltpu.VMEM((CHUNKS, tc, 256), F32),
        pltpu.VMEM((CHUNKS, NY, tc, 128), BF16),
        pltpu.VMEM((512, 256), BF16),
        pltpu.VMEM((tokens, 128), BF16),
        pltpu.VMEM((tokens, 128), BF16),
        dma((3,)),
        dma,
        dma,
        dma,
        dma,
        dma,
        dma,
        dma,
        dma,
        dma,
        dma,
        dma,
        dma((CHUNKS,)),
        dma((CHUNKS,)),
        dma((CHUNKS,)),
        dma((CHUNKS,)),
        dma((CHUNKS,)),
        dma((CHUNKS,)),
        dma((CHUNKS,)),
        dma((CHUNKS,)),
        dma((CHUNKS,)),
    ]
    out = pl.pallas_call(
        kernel,
        out_shape=jax.ShapeDtypeStruct((tokens, 128), BF16),
        in_specs=[smem, smem] + [vmem] * 8,
        out_specs=vmem,
        scratch_shapes=scratch,
        compiler_params=pltpu.CompilerParams(
            collective_id=0, has_side_effects=True, vmem_limit_bytes=60 * 1024 * 1024
        ),
        name="prefill",
    )(
        images,
        texts,
        text_embed,
        patch,
        mw,
        bias.reshape(1, 128),
        gain,
        wq.reshape(NZ, NY, 2, 128, 128),
        jnp.swapaxes(wk[0], 0, 1),
        jnp.swapaxes(wv[0], 0, 1),
    )
    return out[None]


def solution(mesh):
    in_specs = (
        P(None, ("seq", "mp")),
        P(("section", "seq", "mp"), None),
        P(None, ("seq", "mp")),
        P(("seq", "mp")),
        P("section", None),
        P("section", None, ("seq", "mp")),
        P("section", None, ("seq", "mp")),
        P("section", None, ("seq", "mp")),
        P(),
        P(),
    )
    out_specs = P("section", None, ("seq", "mp"))
    return jax.shard_map(shards, mesh=mesh, in_specs=in_specs, out_specs=out_specs, check_vma=False)
```

time: 1030 us -> 161 us (0.16); the launches traced: 1020 us -> 160 us
  blocking collectives: 553 us -> 0 us
  waiting for transfers between devices: 378 us -> 0 us
  Pallas kernels: 0 us -> 158 us
  matrix products: 30.4 us -> 0 us
  other arithmetic: 24.1 us -> 0 us
  between operations: 14.2 us -> 0.01 us
    all_gather x12 -> x0, blocking collectives: 553 us -> none  [the longest x5 248 us: shards(): lax.all_gather(key_part, ('seq', 'mp'), axis=1, tiled=True)]
    all_gather x5 -> x0, waiting for transfers between devices: 364 us -> none  [shards(): whole = lax.all_gather(current, ('seq', 'mp'), axis=1, tiled=True)]
    pallas_call x0 -> x1, Pallas kernels: none -> 158 us  [shards(): pl.pallas_call(kernel, out_shape=jax.ShapeDtypeStruct((tokens, 128), BF16...]
    dot_general x21 -> x0, matrix products: 30.4 us -> none  [the longest x5 14.2 us: shards(): jnp.einsum('qngd,knd->ngqk', query.reshape(rows, local_groups, shared_hea...]
    ppermute x4 -> x0, waiting for transfers between devices: 13.8 us -> none  [from_behind(): return lax.ppermute(block, axis, route)]
    reduce_sum x12 -> x0, other arithmetic: 13.8 us -> none  [the longest x5 12.5 us: shards(): scale = lax.rsqrt(jnp.mean(xf * xf, axis=1, keepdims=True) + 1e-06)]
  transfers between devices with their start and end apart: 9 -> 0, of which waited for: 9 -> 0; matrix products, arithmetic and copies ran while one was open for 0% -> 0% of each run, Pallas kernels for 0% -> 0%
where the time goes in v1:
time: 161 us; the launch traced here: 160 us
  Pallas kernels  158 us (98%)
    pallas_call x1, Pallas kernels, shards(): pl.pallas_call(kernel, out_shape=jax.ShapeDtypeStruct((tokens, 128), BF16...  158 us

profile of v1, /device:TPU:39, one launch (start us, length us, event | category | flops | bytes accessed | tf_op | source)
XLA Modules:
  0.0 159.9 jit_solution(1552453890863544543)
XLA Ops:
  0.0 158.3 %prefill.1 = bf16[320,128]{1,0:T(8,128)(2,1)} custom-call(s32[2,4]{1,0:T(2,128)} %images_ref.1, s32[2,4]{1,0:T(2,128)} %texts_ref.1, bf16[320,128]{1,0:T(8,128)(2,1)} %text_ref.1, bf16[1,5120]{1,0:T(2,128)(2,1)} %patch_ref.1, bf16[5120,128]{1,0:T(8,128)(2,1)} %mw_ref.1, bf16[1,128]{1,0:T(2,128)(2,1)} %bitcast.13, bf16[1,8192]{1,0:T(2,128)(2,1)} %gain_ref.1, ...), custom_call_target="tpu_custom_call" | custom-call | tf_op jit(solution)/shard_map/prefill/pallas_call | solution.py:419
  158.4 1.5 copy.12

commit v2 on v1

--- a/solution.py
+++ b/solution.py
@@ -57,16 +57,21 @@
     kvtx,
     kvrx,
     kvrows,
-    kvmine,
+    kvall,
+    wq_own,
     wq_sib,
+    mw_here,
     weights,
     states,
     xs,
     xr,
     kvx,
     spread,
+    order,
     keys,
     values,
+    l_wq,
+    l_mw,
     s_act,
     r_act1,
     r_act2,
@@ -128,12 +133,18 @@
     def _():
         for dz in (0,) + Z_ORDER:
             greet(at_z(dz, sec - 1))
+        for dy in (2, 1, 3):
+            greet((sec, z * NY + (y + dy) % NY, 1 - core))
 
     @pl.when(sec == 0)
     def _():
         for other in (1, 2, 3):
             greet((other, seq, core))
 
+    load_wq = pltpu.make_async_copy(wq_ref, wq_own, l_wq)
+    load_wq.start()
+    load_mw = pltpu.make_async_copy(mw_ref, mw_here, l_mw)
+    load_mw.start()
     for k in range(40):
         actf[k : k + 1, :] = patch_ref[:, k * 128 : (k + 1) * 128].astype(F32)
     xa = actf[...]
@@ -152,14 +163,25 @@
             lanes = slice((4 * t + b) * 128, (4 * t + b + 1) * 128)
             pieces += [wk_ref[:, lanes], wv_ref[:, lanes]]
         kvtx[:, t] = dot(deal, jnp.concatenate(pieces, axis=0)).astype(BF16).reshape(NZ, 16, 128)
-    for q in range(32):
-        kvmine[q // NY, q % NY, 2] = jnp.zeros((32, 128), BF16)
-        kvmine[q // NY, q % NY, 3] = jnp.zeros((32, 128), BF16)
     r_i, c_i = iota((512, 256), 0), iota((512, 256), 1)
     lane = r_i & 127
     feature = 2 * ((lane & 7) * 8 + (r_i >> 7) * 2 + ((lane >> 5) & 1)) + ((lane >> 3) & 1)
     natural = (lane < 64) & (c_i == ((lane >> 4) & 1) * 128 + feature)
     spread[...] = jnp.where(natural, 1.0, 0.0).astype(BF16)
+    r_i, c_i = iota((256, 256), 0), iota((256, 256), 1)
+    feature = 2 * ((r_i & 7) * 8 + (r_i >> 5)) + ((r_i >> 3) & 1)
+    order[...] = jnp.where(c_i == ((r_i >> 4) & 1) * 128 + feature, 1.0, 0.0).astype(BF16)
+
+    def gain_of(q):
+        g = gains[pl.ds(2 * q + core, 1), :]
+        return jnp.where(iota((128, 128), 0) == iota((128, 128), 1), g, 0.0).astype(BF16)
+
+    load_wq.wait()
+
+    @pl.loop(0, NZ)
+    def _(zz):
+        for yy in range(NY):
+            weights[zz, yy, :, 0:128] = dot(gain_of(zz * NY + yy), wq_own[zz, yy, core]).astype(BF16)
 
     @pl.when(sec == 0)
     def _():
@@ -167,26 +189,16 @@
 
     @pl.when((sec > 0) & (sec < depth - 1))
     def _():
-        pl.semaphore_wait(barrier, 20)
+        pl.semaphore_wait(barrier, 23)
 
     @pl.when(sec == depth - 1)
     def _():
-        pl.semaphore_wait(barrier, 12)
+        pl.semaphore_wait(barrier, 15)
 
     for dz in Z_ORDER:
         send(act, rows.at[core, z, y], s_act.at[0], r_act1, at_z(dz))
     pltpu.make_async_copy(act, rows.at[core, z, y], r_act1).start()
-    send(wq_ref.at[:, :, 1 - core], wq_sib, s_wq, r_wq, sibling)
-
-    def scaled(q, w):
-        g = gains[pl.ds(2 * q + core, 1), :]
-        d = jnp.where(iota((128, 128), 0) == iota((128, 128), 1), g, 0.0).astype(BF16)
-        return d, dot(d, w).astype(BF16)
-
-    @pl.loop(0, 32)
-    def _(q):
-        zz, yy = q // NY, q % NY
-        weights[zz, yy, :, 0:128] = scaled(q, wq_ref[zz, yy, core])[1]
+    send(wq_own.at[:, :, 1 - core], wq_sib, s_wq, r_wq, sibling)
 
     drain(rows.at[core, :, 0], r_act1)
     for i, dy in enumerate((2, 1, 3)):
@@ -197,10 +209,10 @@
 
     drain(wq_sib, r_wq)
 
-    @pl.loop(0, 32)
-    def _(q):
-        zz, yy = q // NY, q % NY
-        weights[zz, yy, :, 128:256] = scaled(q, wq_sib[zz, yy])[1]
+    @pl.loop(0, NZ)
+    def _(zz):
+        for yy in range(NY):
+            weights[zz, yy, :, 128:256] = dot(gain_of(zz * NY + yy), wq_sib[zz, yy]).astype(BF16)
 
     drain(rows.at[core, :, pl.ds(0, 3)], r_act2)
     send(rows.at[core], rows.at[core], s_act.at[2], r_act3, sibling)
@@ -211,17 +223,22 @@
             for yy in range(NY):
                 at = ((p * NZ + zz) * NY + yy) * 40
                 rowsf[at : at + 40, :] = rows[p, zz, yy].astype(F32)
+    load_mw.wait()
     acc = jnp.broadcast_to(bias_ref[...].astype(F32), (64, 128))
     for k in range(20):
         xk = jnp.concatenate(
             [rowsf[pl.ds(2 * k, 64, stride=40), :], rowsf[pl.ds(2 * k + 1, 64, stride=40), :]], axis=1
         ).astype(BF16)
-        acc = acc + dot(xk, mw_ref[256 * k : 256 * (k + 1), :])
+        acc = acc + dot(xk, mw_here[256 * k : 256 * (k + 1), :])
     part[...] = acc.astype(BF16)
 
-    @pl.when(sec > 0)
-    def _():
-        send(part, merged.at[sec], s_part, r_part, (0, seq, core))
+    @pl.when(sec == 1)
+    def _():
+        send(part, merged.at[1], s_part, r_part.at[0], (0, seq, core))
+
+    @pl.when(sec > 1)
+    def _():
+        send(part, merged.at[sec], s_part, r_part.at[1], (0, seq, core))
 
     def place(rows_here, first):
         pos = first + iota((rows_here, 1), 0)
@@ -239,23 +256,37 @@
                 at, seen = at + image + text, seen + image
         return pos, begin, count, earlier
 
-    @pl.when(sec == 0)
-    def _():
-        merged[0] = part[...]
-        pos, begin, count, earlier = place(tokens, 0)
+    def begin_batch(m):
+        first, count_here = m * batch, batch
+        pos, begin, count, earlier = place(count_here, first)
         offset = pos - begin
         is_image = (offset >= 1) & (offset <= count)
-        row = earlier + offset - 1
-        slot = (row & ~63) + ((row & 1) << 5) + ((row & 63) >> 1)
-        chosen = (iota((tokens, 256), 1) == slot) & is_image
-        drain(merged.at[pl.ds(1, 3)], r_part)
-        picked = dot(jnp.where(chosen, 1.0, 0.0).astype(BF16), merged[...].reshape(256, 128))
-        start[...] = jnp.where(is_image, picked, text_ref[...].astype(F32)).astype(BF16)
-        for t in range(CHUNKS):
+        row = earlier + offset - 1 - m * 128
+        slot = (row & 64) + ((row & 1) << 5) + ((row & 63) >> 1)
+        chosen = (iota((count_here, 128), 1) == slot) & is_image
+        picked = dot(
+            jnp.where(chosen, 1.0, 0.0).astype(BF16), merged[2 * m : 2 * m + 2].reshape(128, 128)
+        )
+        text = text_ref[first : first + batch, :].astype(F32)
+        start[first : first + batch, :] = jnp.where(is_image, picked, text).astype(BF16)
+        for t in range(m * per_batch, (m + 1) * per_batch):
             src = start.at[pl.ds(t * tc, tc)]
             for dz in Z_ORDER:
                 send(src, states.at[t, z, y], s_init.at[t], r_st.at[t], at_z(dz))
             pltpu.make_async_copy(src, states.at[t, z, y], r_st.at[t]).start()
+
+    def forward(t):
+        drain(states.at[t, :, 0], r_st.at[t])
+        for dy in (2, 1, 3):
+            send(states.at[t, :, y], states.at[t, :, y], s_fw.at[t], r_fw.at[t], at_y(dy))
+
+    @pl.when(sec == 0)
+    def _():
+        merged[0] = part[...]
+        drain(merged.at[1], r_part.at[0])
+        begin_batch(0)
+        drain(merged.at[pl.ds(2, 2)], r_part.at[1])
+        begin_batch(1)
 
     drain(kvrx, r_kv)
     r_i, c_i = iota((128, 128), 0), iota((128, 128), 1)
@@ -265,35 +296,49 @@
         made = dot(collect, kvrx[:, t].reshape(128, 128)).astype(BF16).reshape(2, 2, 32, 128)
         for h in range(2):
             kvrows[t // 2, (t % 2) * 2 + h] = made[h]
-    send(kvrows.at[:, :, 1 - core], kvmine.at[:, :, core], s_kvm, r_kvm, sibling)
-    mine = pltpu.make_async_copy(kvrows.at[:, :, core], kvmine.at[:, :, core], s_kvm)
-    mine.start()
-
-    def forward(t):
-        drain(states.at[t, :, 0], r_st.at[t])
+
+    @pl.when(sec == 0)
+    def _():
+        send(kvrows.at[:, :, 1 - core], kvall.at[:, :, core], s_kvm, r_kvm, sibling)
+        pltpu.make_async_copy(kvrows.at[:, :, core], kvall.at[:, :, core], r_kvm).start()
+        forward(0)
+        drain(kvall.at[:, :, pl.ds(0, 2)], r_kvm)
+
+        @pl.loop(0, NZ)
+        def _(zz):
+            for yy in range(NY):
+                mine = kvall[zz, yy, 0:2].reshape(64, 128)
+                made = dot_t(gain_of(zz * NY + yy), mine)
+                made = jnp.concatenate([made, jnp.zeros((128, 192), F32)], axis=1)
+                weights[zz, yy, :, 256:512] = made.astype(BF16)
+
+    @pl.when(sec > 0)
+    def _():
+        slot = 2 * y + core
         for dy in (2, 1, 3):
-            send(states.at[t, :, y], states.at[t, :, y], s_fw.at[t], r_fw.at[t], at_y(dy))
-
-    forward(0)
-    drain(kvmine.at[:, :, 0], r_kvm)
-    drain(kvmine.at[:, :, pl.ds(0, 2)], s_kvm)
-
-    @pl.loop(0, 32)
-    def _(q):
-        zz, yy = q // NY, q % NY
-        g = gains[pl.ds(2 * q + core, 1), :]
-        d = jnp.where(iota((128, 128), 0) == iota((128, 128), 1), g, 0.0).astype(BF16)
-        weights[zz, yy, :, 256:384] = dot_t(d, kvmine[zz, yy].reshape(128, 128)).astype(BF16)
+            for other in (core, 1 - core):
+                to = (sec, z * NY + (y + dy) % NY, other)
+                send(kvrows.at[:, :, other], kvall.at[:, :, slot], s_kvm, r_kvm, to)
+        send(kvrows.at[:, :, 1 - core], kvall.at[:, :, slot], s_kvm, r_kvm, sibling)
+        pltpu.make_async_copy(kvrows.at[:, :, core], kvall.at[:, :, slot], r_kvm).start()
+        drain(kvall, r_kvm)
+
+        @pl.loop(0, NZ)
+        def _(zz):
+            for yy in range(NY):
+                made = dot_t(gain_of(zz * NY + yy), kvall[zz, yy].reshape(256, 128)).astype(BF16)
+                weights[zz, yy, :, 256:512] = dot(made, order[...]).astype(BF16)
+
+        forward(0)
 
     for t in range(CHUNKS):
-        if t + 1 < CHUNKS:
-            forward(t + 1)
+        here = slice(t * tc, (t + 1) * tc)
         drain(states.at[t, :, pl.ds(0, 3)], r_fw.at[t])
 
         def products(zz, carry):
             acc, squares = carry
             x = jnp.concatenate([states[t, zz, yy] for yy in range(NY)], axis=1)
-            acc = acc + dot(x, weights[zz].reshape(NY * 128, 384))
+            acc = acc + dot(x, weights[zz].reshape(NY * 128, 512))
             xf = x.astype(F32)
             for yy in range(NY):
                 piece = xf[:, yy * 128 : (yy + 1) * 128]
@@ -301,31 +346,49 @@
             return acc, squares
 
         acc, squares = lax.fori_loop(
-            0, NZ, products, (jnp.zeros((tc, 384), F32), jnp.zeros((tc, 128), F32)), unroll=2
+            0, NZ, products, (jnp.zeros((tc, 512), F32), jnp.zeros((tc, 128), F32)), unroll=2
         )
-        total = jnp.sum(squares, axis=1, keepdims=True)
-        low = iota((tc, 128), 1) < 64
-        mixed = jnp.where(low, acc[:, 256:384], total)
+        total = jnp.broadcast_to(jnp.sum(squares, axis=1, keepdims=True), (tc, 128))
+        own_q, own_kv = acc[:, 0:128], acc[:, 256:512]
         xs[t, :, 0:128] = acc[:, 128:256]
-        xs[t, :, 128:256] = mixed
+        xs[t, :, 128:384] = own_kv
+        xs[t, :, 384:512] = total
         send(xs.at[t], xr.at[t], s_x.at[t], r_x.at[t], sibling)
-        own = acc[:, 0:128]
         pos, begin, _, _ = place(tc, t * tc)
+
+        if t + 1 < CHUNKS:
+
+            @pl.when(sec > 0)
+            def _():
+                forward(t + 1)
+
         drain(xr.at[t], r_x.at[t])
-        mixed = mixed + xr[t, :, 128:256]
-        scale = lax.rsqrt(mixed[:, 64:65] * (1.0 / 8192.0) + 1e-6)
-        kvx[t, y] = jnp.where(low, mixed * scale, 0.0).astype(BF16)
-        for dy in (2, 1, 3):
-            send(kvx.at[t, y], kvx.at[t, y], s_kx.at[t], r_kx.at[t], at_y(dy))
-        query = ((own + xr[t, :, 0:128]) * scale).astype(BF16)
+        scale = lax.rsqrt((total + xr[t, :, 384:512]) * (1.0 / 8192.0) + 1e-6)
+        scales = jnp.concatenate([scale, scale], axis=1)
+        kv = ((own_kv + xr[t, :, 128:384]) * scales).astype(BF16)
+        query = ((own_q + xr[t, :, 0:128]) * scale).astype(BF16)
+
+        @pl.when(sec > 0)
+        def _():
+            keys[here, :] = kv[:, 0:128]
+            values[here, :] = kv[:, 128:256]
+
+        @pl.when(sec == 0)
+        def _():
+            kvx[t, y] = kv[:, 0:128]
+            for dy in (2, 1, 3):
+                send(kvx.at[t, y], kvx.at[t, y], s_kx.at[t], r_kx.at[t], at_y(dy))
+            if t + 1 < CHUNKS:
+                forward(t + 1)
+            drain(kvx.at[t, pl.ds(0, 3)], r_kx.at[t])
+            spread_kv = dot(jnp.concatenate([kvx[t, yy] for yy in range(NY)], axis=1), spread[...])
+            keys[here, :] = spread_kv[:, 0:128].astype(BF16)
+            values[here, :] = spread_kv[:, 128:256].astype(BF16)
+
         first = (t // per_batch) * batch
         span = (t % per_batch + 1) * tc
         column = first + iota((tc, span), 1)
         allowed = (column >= begin) & (column <= pos)
-        drain(kvx.at[t, pl.ds(0, 3)], r_kx.at[t])
-        kv = dot(jnp.concatenate([kvx[t, yy] for yy in range(NY)], axis=1), spread[...]).astype(BF16)
-        keys[t * tc : (t + 1) * tc, :] = kv[:, 0:128]
-        values[t * tc : (t + 1) * tc, :] = kv[:, 128:256]
         scores = dot_t(query, keys[first : first + span, :]) * (1.0 / math.sqrt(HD))
         scores = jnp.where(allowed, scores, -1e30)
         weight = jnp.exp(scores - jnp.max(scores, axis=1, keepdims=True))
@@ -347,15 +410,21 @@
     drain(wq_sib, s_wq)
     drain(kvrx.at[pl.ds(0, 7)], s_kv)
 
+    @pl.when(sec == 0)
+    def _():
+        drain(kvall.at[:, :, 0], s_kvm)
+
     @pl.when(sec > 0)
     def _():
         drain(part, s_part)
+        drain(kvall.at[:, :, pl.ds(0, 7)], s_kvm)
 
     for t in range(CHUNKS):
 
         @pl.when(sec == 0)
         def _():
             drain(states.at[t, pl.ds(0, 7), 0], s_init.at[t])
+            drain(kvx.at[t, pl.ds(0, 3)], s_kx.at[t])
 
         @pl.when(sec < depth - 1)
         def _():
@@ -363,7 +432,6 @@
 
         drain(states.at[t, :, pl.ds(0, 3)], s_fw.at[t])
         drain(xs.at[t], s_x.at[t])
-        drain(kvx.at[t, pl.ds(0, 3)], s_kx.at[t])
 
 
 def shards(text_embed, patch, mw, bias, gain, wq, wk, wv, images, texts):
@@ -371,6 +439,7 @@
     tc = tokens // CHUNKS
     vmem = pl.BlockSpec(memory_space=pltpu.VMEM)
     smem = pl.BlockSpec(memory_space=pltpu.SMEM)
+    hbm = pl.BlockSpec(memory_space=pl.ANY)
     dma = pltpu.SemaphoreType.DMA
     scratch = [
         pltpu.VMEM((64, 128), F32),
@@ -384,16 +453,21 @@
         pltpu.VMEM((NZ, 16, 16, 128), BF16),
         pltpu.VMEM((NZ, 16, 16, 128), BF16),
         pltpu.VMEM((NZ, NY, 2, 32, 128), BF16),
-        pltpu.VMEM((NZ, NY, 4, 32, 128), BF16),
+        pltpu.VMEM((NZ, NY, 8, 32, 128), BF16),
+        pltpu.VMEM((NZ, NY, 2, 128, 128), BF16),
         pltpu.VMEM((NZ, NY, 128, 128), BF16),
-        pltpu.VMEM((NZ, NY, 128, 384), BF16),
+        pltpu.VMEM(mw.shape, BF16),
+        pltpu.VMEM((NZ, NY, 128, 512), BF16),
         pltpu.VMEM((CHUNKS, NZ, NY, tc, 128), BF16),
-        pltpu.VMEM((CHUNKS, tc, 256), F32),
-        pltpu.VMEM((CHUNKS, tc, 256), F32),
+        pltpu.VMEM((CHUNKS, tc, 512), F32),
+        pltpu.VMEM((CHUNKS, tc, 512), F32),
         pltpu.VMEM((CHUNKS, NY, tc, 128), BF16),
         pltpu.VMEM((512, 256), BF16),
+        pltpu.VMEM((256, 256), BF16),
         pltpu.VMEM((tokens, 128), BF16),
         pltpu.VMEM((tokens, 128), BF16),
+        dma,
+        dma,
         dma((3,)),
         dma,
         dma,
@@ -405,7 +479,7 @@
         dma,
         dma,
         dma,
-        dma,
+        dma((2,)),
         dma((CHUNKS,)),
         dma((CHUNKS,)),
         dma((CHUNKS,)),
@@ -419,7 +493,7 @@
     out = pl.pallas_call(
         kernel,
         out_shape=jax.ShapeDtypeStruct((tokens, 128), BF16),
-        in_specs=[smem, smem] + [vmem] * 8,
+        in_specs=[smem, smem, vmem, vmem, hbm, vmem, vmem, hbm, vmem, vmem],
         out_specs=vmem,
         scratch_shapes=scratch,
         compiler_params=pltpu.CompilerParams(

time: 161 us -> 142 us (0.88)
  Pallas kernels: 158 us -> 139 us
    pallas_call x1, Pallas kernels: 158 us -> 139 us  [shards(): pl.pallas_call(kernel, out_shape=jax.ShapeDtypeStruct((tokens, 128), BF16...]
where the time goes in v2:
time: 142 us; the launch traced here: 141 us
  Pallas kernels  139 us (98%)
  local copies, waits for them, and re-layouts  1.53 us (1%)
    pallas_call x1, Pallas kernels, shards(): pl.pallas_call(kernel, out_shape=jax.ShapeDtypeStruct((tokens, 128), BF16...  139 us

profile of v2, /device:TPU:39, one launch (start us, length us, event | category | flops | bytes accessed | tf_op | source)
XLA Modules:
  0.0 141.0 jit_solution(5613886009304697843)
XLA Ops:
  0.0 139.4 %prefill.1 = bf16[320,128]{1,0:T(8,128)(2,1)} custom-call(s32[2,4]{1,0:T(2,128)} %images_ref.1, s32[2,4]{1,0:T(2,128)} %texts_ref.1, bf16[320,128]{1,0:T(8,128)(2,1)} %text_ref.1, bf16[1,5120]{1,0:T(2,128)(2,1)} %patch_ref.1, bf16[5120,128]{1,0:T(8,128)(2,1)} %mw_ref.1, bf16[1,128]{1,0:T(2,128)(2,1)} %bitcast.13, bf16[1,8192]{1,0:T(2,128)(2,1)} %gain_ref.1, ...), custom_call_target="tpu_custom_call" | custom-call | tf_op jit(solution)/shard_map/prefill/pallas_call | solution.py:493
  139.5 1.5 %copy.12 = bf16[1,320,128]{2,1,0:T(8,128)(2,1)} copy(bf16[1,320,128]{2,1,0:T(8,128)(2,1)} %bitcast.10) | data formatting | bytes 163840

commit v3 on v2

--- a/solution.py
+++ b/solution.py
@@ -16,6 +16,7 @@
 NZ = 8
 CHUNKS = 4
 Z_ORDER = (4, 3, 5, 2, 6, 1, 7)
+CLASSES = ((0, 1, 7, 2), (6, 3, 5, 4))
 
 
 def iota(shape, dim):
@@ -68,6 +69,7 @@
     kvx,
     spread,
     order,
+    queries,
     keys,
     values,
     l_wq,
@@ -82,13 +84,16 @@
     r_kv,
     s_kvm,
     r_kvm,
+    r_kvn,
+    r_kvf,
     s_part,
     r_part,
     s_init,
     s_st,
     r_st,
     s_fw,
-    r_fw,
+    r_near,
+    r_far,
     s_x,
     r_x,
     s_kx,
@@ -103,7 +108,6 @@
     tokens = out_ref.shape[0]
     tc = tokens // CHUNKS
     batch = tokens // images_ref.shape[0]
-    per_batch = batch // tc
 
     def at_z(dz, s=None):
         return (sec if s is None else s, ((z + dz) % NZ) * NY + y, core)
@@ -133,7 +137,7 @@
     def _():
         for dz in (0,) + Z_ORDER:
             greet(at_z(dz, sec - 1))
-        for dy in (2, 1, 3):
+        for dy in (1, 3):
             greet((sec, z * NY + (y + dy) % NY, 1 - core))
 
     @pl.when(sec == 0)
@@ -189,23 +193,27 @@
 
     @pl.when((sec > 0) & (sec < depth - 1))
     def _():
-        pl.semaphore_wait(barrier, 23)
+        pl.semaphore_wait(barrier, 22)
 
     @pl.when(sec == depth - 1)
     def _():
-        pl.semaphore_wait(barrier, 15)
+        pl.semaphore_wait(barrier, 14)
 
     for dz in Z_ORDER:
         send(act, rows.at[core, z, y], s_act.at[0], r_act1, at_z(dz))
     pltpu.make_async_copy(act, rows.at[core, z, y], r_act1).start()
+
+    def deal_rows():
+        for dz in Z_ORDER:
+            send(kvtx.at[(z + dz) % NZ], kvrx.at[z], s_kv, r_kv, at_z(dz))
+        pltpu.make_async_copy(kvtx.at[z], kvrx.at[z], r_kv).start()
+
     send(wq_own.at[:, :, 1 - core], wq_sib, s_wq, r_wq, sibling)
 
     drain(rows.at[core, :, 0], r_act1)
     for i, dy in enumerate((2, 1, 3)):
         send(rows.at[core, :, y], rows.at[core, :, y], s_act.at[1], r_act2, at_y(dy))
-    for dz in Z_ORDER:
-        send(kvtx.at[(z + dz) % NZ], kvrx.at[z], s_kv, r_kv, at_z(dz))
-    pltpu.make_async_copy(kvtx.at[z], kvrx.at[z], r_kv).start()
+    deal_rows()
 
     drain(wq_sib, r_wq)
 
@@ -269,22 +277,43 @@
         )
         text = text_ref[first : first + batch, :].astype(F32)
         start[first : first + batch, :] = jnp.where(is_image, picked, text).astype(BF16)
-        for t in range(m * per_batch, (m + 1) * per_batch):
-            src = start.at[pl.ds(t * tc, tc)]
-            for dz in Z_ORDER:
-                send(src, states.at[t, z, y], s_init.at[t], r_st.at[t], at_z(dz))
-            pltpu.make_async_copy(src, states.at[t, z, y], r_st.at[t]).start()
+
+    def begin_chunk(t):
+        src = start.at[pl.ds(t * tc, tc)]
+        for k in range(2):
+            for dz in CLASSES[k]:
+                if dz:
+                    send(src, states.at[t, z, y], s_init.at[t], r_st.at[t, k], at_z(dz))
+        pltpu.make_async_copy(src, states.at[t, z, y], r_st.at[t, 0]).start()
+
+    def from_z(t, dz, yy):
+        return states.at[t, (z + NZ - dz) % NZ, yy % NY]
 
     def forward(t):
-        drain(states.at[t, :, 0], r_st.at[t])
-        for dy in (2, 1, 3):
-            send(states.at[t, :, y], states.at[t, :, y], s_fw.at[t], r_fw.at[t], at_y(dy))
+        for k in range(2):
+            drain(states.at[t, pl.ds(0, 4), 0], r_st.at[t, k])
+            for dz in CLASSES[k]:
+                block = from_z(t, dz, y)
+                send(block, block, s_fw.at[t], r_near.at[t, k, 0], at_y(1))
+                send(block, block, s_fw.at[t], r_near.at[t, k, 1], at_y(3))
+
+    def pass_on(t):
+        for k in range(2):
+            drain(states.at[t, pl.ds(0, 4), 0], r_near.at[t, k, 0])
+            for dz in CLASSES[k][:2]:
+                block = from_z(t, dz, y + 3)
+                send(block, block, s_fw.at[t], r_far.at[t], at_y(1))
+            drain(states.at[t, pl.ds(0, 4), 0], r_near.at[t, k, 1])
+            for dz in CLASSES[k][2:]:
+                block = from_z(t, dz, y + 1)
+                send(block, block, s_fw.at[t], r_far.at[t], at_y(3))
 
     @pl.when(sec == 0)
     def _():
         merged[0] = part[...]
         drain(merged.at[1], r_part.at[0])
         begin_batch(0)
+        begin_chunk(0)
         drain(merged.at[pl.ds(2, 2)], r_part.at[1])
         begin_batch(1)
 
@@ -302,6 +331,7 @@
         send(kvrows.at[:, :, 1 - core], kvall.at[:, :, core], s_kvm, r_kvm, sibling)
         pltpu.make_async_copy(kvrows.at[:, :, core], kvall.at[:, :, core], r_kvm).start()
         forward(0)
+        begin_chunk(1)
         drain(kvall.at[:, :, pl.ds(0, 2)], r_kvm)
 
         @pl.loop(0, NZ)
@@ -315,13 +345,20 @@
     @pl.when(sec > 0)
     def _():
         slot = 2 * y + core
-        for dy in (2, 1, 3):
+        for i, dy in enumerate((1, 3)):
             for other in (core, 1 - core):
                 to = (sec, z * NY + (y + dy) % NY, other)
-                send(kvrows.at[:, :, other], kvall.at[:, :, slot], s_kvm, r_kvm, to)
+                send(kvrows.at[:, :, other], kvall.at[:, :, slot], s_kvm, r_kvn.at[i], to)
         send(kvrows.at[:, :, 1 - core], kvall.at[:, :, slot], s_kvm, r_kvm, sibling)
         pltpu.make_async_copy(kvrows.at[:, :, core], kvall.at[:, :, slot], r_kvm).start()
-        drain(kvall, r_kvm)
+        drain(kvall.at[:, :, pl.ds(0, 2)], r_kvn.at[0])
+        below = kvall.at[:, :, 2 * ((y + 3) % NY) + 1]
+        send(below, below, s_kvm, r_kvf, at_y(1))
+        drain(kvall.at[:, :, pl.ds(0, 2)], r_kvn.at[1])
+        above = kvall.at[:, :, 2 * ((y + 1) % NY)]
+        send(above, above, s_kvm, r_kvf, at_y(3))
+        drain(kvall.at[:, :, pl.ds(0, 2)], r_kvm)
+        drain(kvall.at[:, :, pl.ds(0, 2)], r_kvf)
 
         @pl.loop(0, NZ)
         def _(zz):
@@ -331,10 +368,7 @@
 
         forward(0)
 
-    for t in range(CHUNKS):
-        here = slice(t * tc, (t + 1) * tc)
-        drain(states.at[t, :, pl.ds(0, 3)], r_fw.at[t])
-
+    def project(t):
         def products(zz, carry):
             acc, squares = carry
             x = jnp.concatenate([states[t, zz, yy] for yy in range(NY)], axis=1)
@@ -354,55 +388,81 @@
         xs[t, :, 128:384] = own_kv
         xs[t, :, 384:512] = total
         send(xs.at[t], xr.at[t], s_x.at[t], r_x.at[t], sibling)
-        pos, begin, _, _ = place(tc, t * tc)
-
-        if t + 1 < CHUNKS:
-
-            @pl.when(sec > 0)
-            def _():
-                forward(t + 1)
-
         drain(xr.at[t], r_x.at[t])
         scale = lax.rsqrt((total + xr[t, :, 384:512]) * (1.0 / 8192.0) + 1e-6)
         scales = jnp.concatenate([scale, scale], axis=1)
         kv = ((own_kv + xr[t, :, 128:384]) * scales).astype(BF16)
-        query = ((own_q + xr[t, :, 0:128]) * scale).astype(BF16)
-
-        @pl.when(sec > 0)
-        def _():
-            keys[here, :] = kv[:, 0:128]
-            values[here, :] = kv[:, 128:256]
-
-        @pl.when(sec == 0)
-        def _():
-            kvx[t, y] = kv[:, 0:128]
-            for dy in (2, 1, 3):
-                send(kvx.at[t, y], kvx.at[t, y], s_kx.at[t], r_kx.at[t], at_y(dy))
-            if t + 1 < CHUNKS:
-                forward(t + 1)
-            drain(kvx.at[t, pl.ds(0, 3)], r_kx.at[t])
-            spread_kv = dot(jnp.concatenate([kvx[t, yy] for yy in range(NY)], axis=1), spread[...])
-            keys[here, :] = spread_kv[:, 0:128].astype(BF16)
-            values[here, :] = spread_kv[:, 128:256].astype(BF16)
-
-        first = (t // per_batch) * batch
-        span = (t % per_batch + 1) * tc
+        queries[t] = ((own_q + xr[t, :, 0:128]) * scale).astype(BF16)
+        return kv
+
+    def attend(t):
+        here = slice(t * tc, (t + 1) * tc)
+        first = (t * tc // batch) * batch
+        span = (t + 1) * tc - first
+        pos, begin, _, _ = place(tc, t * tc)
         column = first + iota((tc, span), 1)
         allowed = (column >= begin) & (column <= pos)
-        scores = dot_t(query, keys[first : first + span, :]) * (1.0 / math.sqrt(HD))
+        scores = dot_t(queries[t], keys[first : first + span, :]) * (1.0 / math.sqrt(HD))
         scores = jnp.where(allowed, scores, -1e30)
         weight = jnp.exp(scores - jnp.max(scores, axis=1, keepdims=True))
         probs = (weight / jnp.sum(weight, axis=1, keepdims=True)).astype(BF16)
         attended = dot(probs, values[first : first + span, :])
         state = states[t, z, y].astype(F32) + attended
-        out_ref[t * tc : (t + 1) * tc, :] = state.astype(BF16)
+        out_ref[here, :] = state.astype(BF16)
 
         @pl.when(sec < depth - 1)
         def _():
-            for dz in Z_ORDER + (0,):
-                send(
-                    out_ref.at[pl.ds(t * tc, tc)], states.at[t, z, y], s_st.at[t], r_st.at[t], at_z(dz, sec + 1)
-                )
+            for k in range(2):
+                for dz in CLASSES[k]:
+                    send(
+                        out_ref.at[pl.ds(t * tc, tc)],
+                        states.at[t, z, y],
+                        s_st.at[t],
+                        r_st.at[t, k],
+                        at_z(dz, sec + 1),
+                    )
+
+    def attend_shared(t):
+        here = slice(t * tc, (t + 1) * tc)
+        drain(kvx.at[t, pl.ds(0, 3)], r_kx.at[t])
+        kv = dot(jnp.concatenate([kvx[t, yy] for yy in range(NY)], axis=1), spread[...]).astype(BF16)
+        keys[here, :] = kv[:, 0:128]
+        values[here, :] = kv[:, 128:256]
+        attend(t)
+
+    @pl.when(sec == 0)
+    def _():
+        def next_chunk(t):
+            if t < CHUNKS:
+                forward(t)
+            if t + 1 < CHUNKS:
+                begin_chunk(t + 1)
+
+        pass_on(0)
+        next_chunk(1)
+        for t in range(CHUNKS):
+            drain(states.at[t, :, 0], r_far.at[t])
+            kv = project(t)
+            kvx[t, y] = kv[:, 0:128]
+            for dy in (2, 1, 3):
+                send(kvx.at[t, y], kvx.at[t, y], s_kx.at[t], r_kx.at[t], at_y(dy))
+            if t + 1 < CHUNKS:
+                pass_on(t + 1)
+            next_chunk(t + 2)
+            attend_shared(t)
+
+    @pl.when(sec > 0)
+    def _():
+        for t in range(CHUNKS):
+            here = slice(t * tc, (t + 1) * tc)
+            pass_on(t)
+            if t + 1 < CHUNKS:
+                forward(t + 1)
+            drain(states.at[t, :, 0], r_far.at[t])
+            kv = project(t)
+            keys[here, :] = kv[:, 0:128]
+            values[here, :] = kv[:, 128:256]
+            attend(t)
 
     drain(rows.at[core, pl.ds(0, 7), 0], s_act.at[0])
     drain(rows.at[core, :, pl.ds(0, 3)], s_act.at[1])
@@ -464,6 +524,7 @@
         pltpu.VMEM((CHUNKS, NY, tc, 128), BF16),
         pltpu.VMEM((512, 256), BF16),
         pltpu.VMEM((256, 256), BF16),
+        pltpu.VMEM((CHUNKS, tc, 128), BF16),
         pltpu.VMEM((tokens, 128), BF16),
         pltpu.VMEM((tokens, 128), BF16),
         dma,
@@ -478,12 +539,15 @@
         dma,
         dma,
         dma,
-        dma,
         dma((2,)),
-        dma((CHUNKS,)),
-        dma((CHUNKS,)),
-        dma((CHUNKS,)),
-        dma((CHUNKS,)),
+        dma,
+        dma,
+        dma((2,)),
+        dma((CHUNKS,)),
+        dma((CHUNKS,)),
+        dma((CHUNKS, 2)),
+        dma((CHUNKS,)),
+        dma((CHUNKS, 2, 2)),
         dma((CHUNKS,)),
         dma((CHUNKS,)),
         dma((CHUNKS,)),

time: 142 us -> 126 us (0.89)
  Pallas kernels: 139 us -> 124 us
    pallas_call x1, Pallas kernels: 139 us -> 124 us  [shards(): pl.pallas_call(kernel, out_shape=jax.ShapeDtypeStruct((tokens, 128), BF16...]
where the time goes in v3:
time: 126 us
  Pallas kernels  124 us (98%)
  local copies, waits for them, and re-layouts  1.53 us (1%)
    pallas_call x1, Pallas kernels, shards(): pl.pallas_call(kernel, out_shape=jax.ShapeDtypeStruct((tokens, 128), BF16...  124 us

profile of v3, /device:TPU:39, one launch (start us, length us, event | category | flops | bytes accessed | tf_op | source)
XLA Modules:
  0.0 126.0 jit_solution(4781266199999479688)
XLA Ops:
  0.0 124.5 %prefill.1 = bf16[320,128]{1,0:T(8,128)(2,1)} custom-call(s32[2,4]{1,0:T(2,128)} %images_ref.1, s32[2,4]{1,0:T(2,128)} %texts_ref.1, bf16[320,128]{1,0:T(8,128)(2,1)} %text_ref.1, bf16[1,5120]{1,0:T(2,128)(2,1)} %patch_ref.1, bf16[5120,128]{1,0:T(8,128)(2,1)} %mw_ref.1, bf16[1,128]{1,0:T(2,128)(2,1)} %bitcast.13, bf16[1,8192]{1,0:T(2,128)(2,1)} %gain_ref.1, ...), custom_call_target="tpu_custom_call" | custom-call | tf_op jit(solution)/shard_map/prefill/pallas_call | solution.py:557
  124.5 1.5 %copy.12 = bf16[1,320,128]{2,1,0:T(8,128)(2,1)} copy(bf16[1,320,128]{2,1,0:T(8,128)(2,1)} %bitcast.10) | data formatting | bytes 163840

commit v4 on v3

--- a/solution.py
+++ b/solution.py
@@ -16,7 +16,10 @@
 NZ = 8
 CHUNKS = 4
 Z_ORDER = (4, 3, 5, 2, 6, 1, 7)
-CLASSES = ((0, 1, 7, 2), (6, 3, 5, 4))
+KINDS = 4
+PER_KIND = NZ // KINDS
+VISIT = (0, 1, 3, 2)
+SENDS = (0, 7, 1, 2, 6, 5, 3, 4)
 
 
 def iota(shape, dim):
@@ -208,12 +211,20 @@
             send(kvtx.at[(z + dz) % NZ], kvrx.at[z], s_kv, r_kv, at_z(dz))
         pltpu.make_async_copy(kvtx.at[z], kvrx.at[z], r_kv).start()
 
+
+    @pl.when(sec == 0)
+    def _():
+        deal_rows()
+
     send(wq_own.at[:, :, 1 - core], wq_sib, s_wq, r_wq, sibling)
 
     drain(rows.at[core, :, 0], r_act1)
     for i, dy in enumerate((2, 1, 3)):
         send(rows.at[core, :, y], rows.at[core, :, y], s_act.at[1], r_act2, at_y(dy))
-    deal_rows()
+
+    @pl.when(sec > 0)
+    def _():
+        deal_rows()
 
     drain(wq_sib, r_wq)
 
@@ -278,35 +289,55 @@
         text = text_ref[first : first + batch, :].astype(F32)
         start[first : first + batch, :] = jnp.where(is_image, picked, text).astype(BF16)
 
+    def slot_of(dz):
+        return (dz + 1) % NZ
+
     def begin_chunk(t):
         src = start.at[pl.ds(t * tc, tc)]
-        for k in range(2):
-            for dz in CLASSES[k]:
-                if dz:
-                    send(src, states.at[t, z, y], s_init.at[t], r_st.at[t, k], at_z(dz))
-        pltpu.make_async_copy(src, states.at[t, z, y], r_st.at[t, 0]).start()
-
-    def from_z(t, dz, yy):
-        return states.at[t, (z + NZ - dz) % NZ, yy % NY]
-
-    def forward(t):
-        for k in range(2):
-            drain(states.at[t, pl.ds(0, 4), 0], r_st.at[t, k])
-            for dz in CLASSES[k]:
-                block = from_z(t, dz, y)
-                send(block, block, s_fw.at[t], r_near.at[t, k, 0], at_y(1))
-                send(block, block, s_fw.at[t], r_near.at[t, k, 1], at_y(3))
-
-    def pass_on(t):
-        for k in range(2):
-            drain(states.at[t, pl.ds(0, 4), 0], r_near.at[t, k, 0])
-            for dz in CLASSES[k][:2]:
-                block = from_z(t, dz, y + 3)
-                send(block, block, s_fw.at[t], r_far.at[t], at_y(1))
-            drain(states.at[t, pl.ds(0, 4), 0], r_near.at[t, k, 1])
-            for dz in CLASSES[k][2:]:
-                block = from_z(t, dz, y + 1)
-                send(block, block, s_fw.at[t], r_far.at[t], at_y(3))
+        for dz in SENDS:
+            if dz:
+                send(src, states.at[t, y, slot_of(dz)], s_init.at[t], r_st.at[t, slot_of(dz) // PER_KIND], at_z(dz))
+        pltpu.make_async_copy(src, states.at[t, y, slot_of(0)], r_st.at[t, slot_of(0) // PER_KIND]).start()
+
+    def forward(t, i):
+        k = VISIT[i]
+        drain(states.at[t, 0, pl.ds(0, PER_KIND)], r_st.at[t, k])
+        block = states.at[t, y, pl.ds(k * PER_KIND, PER_KIND)]
+        send(block, block, s_fw.at[t], r_near.at[t, k, 0], at_y(1))
+        send(block, block, s_fw.at[t], r_near.at[t, k, 1], at_y(3))
+
+    def pass_on(t, i):
+        k, half = VISIT[i], PER_KIND // 2
+        drain(states.at[t, 0, pl.ds(0, PER_KIND)], r_near.at[t, k, 0])
+        below = states.at[t, (y + 3) % NY, pl.ds(k * PER_KIND, half)]
+        send(below, below, s_fw.at[t], r_far.at[t], at_y(1))
+        drain(states.at[t, 0, pl.ds(0, PER_KIND)], r_near.at[t, k, 1])
+        above = states.at[t, (y + 1) % NY, pl.ds(k * PER_KIND + half, half)]
+        send(above, above, s_fw.at[t], r_far.at[t], at_y(3))
+
+    def forward_all(t):
+        for k in range(KINDS):
+            forward(t, k)
+
+    def pass_on_all(t):
+        for k in range(KINDS):
+            pass_on(t, k)
+
+    def forward_part(t, part_of):
+        for k in range(part_of * KINDS // 2, (part_of + 1) * KINDS // 2):
+            forward(t, k)
+
+    def pass_on_part(t, part_of):
+        for k in range(part_of * KINDS // 2, (part_of + 1) * KINDS // 2):
+            pass_on(t, k)
+
+    def spread_y(t):
+        for k in range(KINDS):
+            forward(t, k)
+            if k >= 2:
+                pass_on(t, k - 2)
+        for k in range(max(0, KINDS - 2), KINDS):
+            pass_on(t, k)
 
     @pl.when(sec == 0)
     def _():
@@ -330,8 +361,9 @@
     def _():
         send(kvrows.at[:, :, 1 - core], kvall.at[:, :, core], s_kvm, r_kvm, sibling)
         pltpu.make_async_copy(kvrows.at[:, :, core], kvall.at[:, :, core], r_kvm).start()
-        forward(0)
+        forward_part(0, 0)
         begin_chunk(1)
+        forward_part(0, 1)
         drain(kvall.at[:, :, pl.ds(0, 2)], r_kvm)
 
         @pl.loop(0, NZ)
@@ -360,34 +392,56 @@
         drain(kvall.at[:, :, pl.ds(0, 2)], r_kvm)
         drain(kvall.at[:, :, pl.ds(0, 2)], r_kvf)
 
-        @pl.loop(0, NZ)
-        def _(zz):
-            for yy in range(NY):
-                made = dot_t(gain_of(zz * NY + yy), kvall[zz, yy].reshape(256, 128)).astype(BF16)
-                weights[zz, yy, :, 256:512] = dot(made, order[...]).astype(BF16)
-
-        forward(0)
-
-    def project(t):
-        def products(zz, carry):
-            acc, squares = carry
-            x = jnp.concatenate([states[t, zz, yy] for yy in range(NY)], axis=1)
-            acc = acc + dot(x, weights[zz].reshape(NY * 128, 512))
-            xf = x.astype(F32)
-            for yy in range(NY):
-                piece = xf[:, yy * 128 : (yy + 1) * 128]
-                squares = squares + piece * piece
-            return acc, squares
-
-        acc, squares = lax.fori_loop(
-            0, NZ, products, (jnp.zeros((tc, 512), F32), jnp.zeros((tc, 128), F32)), unroll=2
-        )
+        def prepare(low, high):
+            @pl.loop(low, high)
+            def _(zz):
+                for yy in range(NY):
+                    made = dot_t(gain_of(zz * NY + yy), kvall[zz, yy].reshape(256, 128)).astype(BF16)
+                    weights[zz, yy, :, 256:512] = dot(made, order[...]).astype(BF16)
+
+        prepare(0, NZ // 2)
+
+        @pl.when(sec == 1)
+        def _():
+            forward_part(0, 0)
+
+        prepare(NZ // 2, NZ)
+
+        @pl.when(sec == 1)
+        def _():
+            forward_part(0, 1)
+            pass_on_all(0)
+
+        @pl.when(sec > 1)
+        def _():
+            spread_y(0)
+
+    def project(t, meanwhile=lambda: None):
+        def products(ya, yb):
+            def step(slot, carry):
+                acc, squares = carry
+                zz = (z + 2 * NZ + 1 - slot) % NZ
+                x = jnp.concatenate([states[t, ya, slot], states[t, yb, slot]], axis=1)
+                w = jnp.concatenate([weights[zz, ya], weights[zz, yb]], axis=0)
+                acc = acc + dot(x, w)
+                xf = x.astype(F32)
+                for piece in (xf[:, 0:128], xf[:, 128:256]):
+                    squares = squares + piece * piece
+                return acc, squares
+
+            return step
+
+        sums = jnp.zeros((tc, 512), F32), jnp.zeros((tc, 128), F32)
+        sums = lax.fori_loop(0, NZ, products(y, (y + 1) % NY), sums, unroll=4)
+        drain(states.at[t, 0], r_far.at[t])
+        acc, squares = lax.fori_loop(0, NZ, products((y + 2) % NY, (y + 3) % NY), sums, unroll=4)
         total = jnp.broadcast_to(jnp.sum(squares, axis=1, keepdims=True), (tc, 128))
         own_q, own_kv = acc[:, 0:128], acc[:, 256:512]
         xs[t, :, 0:128] = acc[:, 128:256]
         xs[t, :, 128:384] = own_kv
         xs[t, :, 384:512] = total
         send(xs.at[t], xr.at[t], s_x.at[t], r_x.at[t], sibling)
+        meanwhile()
         drain(xr.at[t], r_x.at[t])
         scale = lax.rsqrt((total + xr[t, :, 384:512]) * (1.0 / 8192.0) + 1e-6)
         scales = jnp.concatenate([scale, scale], axis=1)
@@ -407,20 +461,19 @@
         weight = jnp.exp(scores - jnp.max(scores, axis=1, keepdims=True))
         probs = (weight / jnp.sum(weight, axis=1, keepdims=True)).astype(BF16)
         attended = dot(probs, values[first : first + span, :])
-        state = states[t, z, y].astype(F32) + attended
+        state = states[t, y, slot_of(0)].astype(F32) + attended
         out_ref[here, :] = state.astype(BF16)
 
         @pl.when(sec < depth - 1)
         def _():
-            for k in range(2):
-                for dz in CLASSES[k]:
-                    send(
-                        out_ref.at[pl.ds(t * tc, tc)],
-                        states.at[t, z, y],
-                        s_st.at[t],
-                        r_st.at[t, k],
-                        at_z(dz, sec + 1),
-                    )
+            for dz in SENDS:
+                send(
+                    out_ref.at[pl.ds(t * tc, tc)],
+                    states.at[t, y, slot_of(dz)],
+                    s_st.at[t],
+                    r_st.at[t, slot_of(dz) // PER_KIND],
+                    at_z(dz, sec + 1),
+                )
 
     def attend_shared(t):
         here = slice(t * tc, (t + 1) * tc)
@@ -432,34 +485,44 @@
 
     @pl.when(sec == 0)
     def _():
-        def next_chunk(t):
+        def first_half(t):
             if t < CHUNKS:
-                forward(t)
+                forward_part(t, 0)
             if t + 1 < CHUNKS:
                 begin_chunk(t + 1)
 
-        pass_on(0)
-        next_chunk(1)
+        def second_half(t):
+            if t < CHUNKS:
+                forward_part(t, 1)
+
+        pass_on_all(0)
+        first_half(1)
+        second_half(1)
         for t in range(CHUNKS):
-            drain(states.at[t, :, 0], r_far.at[t])
             kv = project(t)
             kvx[t, y] = kv[:, 0:128]
             for dy in (2, 1, 3):
                 send(kvx.at[t, y], kvx.at[t, y], s_kx.at[t], r_kx.at[t], at_y(dy))
             if t + 1 < CHUNKS:
-                pass_on(t + 1)
-            next_chunk(t + 2)
+                pass_on_all(t + 1)
+            first_half(t + 2)
             attend_shared(t)
+            second_half(t + 2)
 
     @pl.when(sec > 0)
     def _():
         for t in range(CHUNKS):
             here = slice(t * tc, (t + 1) * tc)
-            pass_on(t)
+            if t > 0:
+                pass_on_part(t, 1)
             if t + 1 < CHUNKS:
-                forward(t + 1)
-            drain(states.at[t, :, 0], r_far.at[t])
-            kv = project(t)
+                forward_all(t + 1)
+
+            def early():
+                if t + 1 < CHUNKS:
+                    pass_on_part(t + 1, 0)
+
+            kv = project(t, early)
             keys[here, :] = kv[:, 0:128]
             values[here, :] = kv[:, 128:256]
             attend(t)
@@ -483,14 +546,14 @@
 
         @pl.when(sec == 0)
         def _():
-            drain(states.at[t, pl.ds(0, 7), 0], s_init.at[t])
+            drain(states.at[t, 0, pl.ds(0, 7)], s_init.at[t])
             drain(kvx.at[t, pl.ds(0, 3)], s_kx.at[t])
 
         @pl.when(sec < depth - 1)
         def _():
-            drain(states.at[t, :, 0], s_st.at[t])
-
-        drain(states.at[t, :, pl.ds(0, 3)], s_fw.at[t])
+            drain(states.at[t, 0], s_st.at[t])
+
+        drain(states.at[t, pl.ds(0, 3)], s_fw.at[t])
         drain(xs.at[t], s_x.at[t])
 
 
@@ -518,7 +581,7 @@
         pltpu.VMEM((NZ, NY, 128, 128), BF16),
         pltpu.VMEM(mw.shape, BF16),
         pltpu.VMEM((NZ, NY, 128, 512), BF16),
-        pltpu.VMEM((CHUNKS, NZ, NY, tc, 128), BF16),
+        pltpu.VMEM((CHUNKS, NY, NZ, tc, 128), BF16),
         pltpu.VMEM((CHUNKS, tc, 512), F32),
         pltpu.VMEM((CHUNKS, tc, 512), F32),
         pltpu.VMEM((CHUNKS, NY, tc, 128), BF16),
@@ -545,9 +608,9 @@
         dma((2,)),
         dma((CHUNKS,)),
         dma((CHUNKS,)),
-        dma((CHUNKS, 2)),
-        dma((CHUNKS,)),
-        dma((CHUNKS, 2, 2)),
+        dma((CHUNKS, KINDS)),
+        dma((CHUNKS,)),
+        dma((CHUNKS, KINDS, 2)),
         dma((CHUNKS,)),
         dma((CHUNKS,)),
         dma((CHUNKS,)),

time: 126 us -> 120 us (0.952)
  Pallas kernels: 124 us -> 117 us
    pallas_call x1, Pallas kernels: 124 us -> 117 us  [shards(): pl.pallas_call(kernel, out_shape=jax.ShapeDtypeStruct((tokens, 128), BF16...]
where the time goes in v4:
time: 120 us; the launch traced here: 119 us
  Pallas kernels  117 us (98%)
  local copies, waits for them, and re-layouts  1.53 us (1%)
    pallas_call x1, Pallas kernels, shards(): pl.pallas_call(kernel, out_shape=jax.ShapeDtypeStruct((tokens, 128), BF16...  117 us

profile of v4, /device:TPU:39, one launch (start us, length us, event | category | flops | bytes accessed | tf_op | source)
XLA Modules:
  0.0 118.8 jit_solution(7680391412008531460)
XLA Ops:
  0.0 117.2 %prefill.1 = bf16[320,128]{1,0:T(8,128)(2,1)} custom-call(s32[2,4]{1,0:T(2,128)} %images_ref.1, s32[2,4]{1,0:T(2,128)} %texts_ref.1, bf16[320,128]{1,0:T(8,128)(2,1)} %text_ref.1, bf16[1,5120]{1,0:T(2,128)(2,1)} %patch_ref.1, bf16[5120,128]{1,0:T(8,128)(2,1)} %mw_ref.1, bf16[1,128]{1,0:T(2,128)(2,1)} %bitcast.13, bf16[1,8192]{1,0:T(2,128)(2,1)} %gain_ref.1, ...), custom_call_target="tpu_custom_call" | custom-call | tf_op jit(solution)/shard_map/prefill/pallas_call | solution.py:620
  117.2 1.5 %copy.12 = bf16[1,320,128]{2,1,0:T(8,128)(2,1)} copy(bf16[1,320,128]{2,1,0:T(8,128)(2,1)} %bitcast.10) | data formatting | bytes 163840

commit v5 on v4

--- a/solution.py
+++ b/solution.py
@@ -202,9 +202,10 @@
     def _():
         pl.semaphore_wait(barrier, 14)
 
-    for dz in Z_ORDER:
-        send(act, rows.at[core, z, y], s_act.at[0], r_act1, at_z(dz))
-    pltpu.make_async_copy(act, rows.at[core, z, y], r_act1).start()
+    for dz in (1, 7, 2, 6, 3, 5, 4):
+        slot = (dz + 1) % NZ
+        send(act, rows.at[core, y, slot], s_act.at[0], r_act1.at[slot // 4], at_z(dz))
+    pltpu.make_async_copy(act, rows.at[core, y, 1], r_act1.at[0]).start()
 
     def deal_rows():
         for dz in Z_ORDER:
@@ -218,9 +219,11 @@
 
     send(wq_own.at[:, :, 1 - core], wq_sib, s_wq, r_wq, sibling)
 
-    drain(rows.at[core, :, 0], r_act1)
-    for i, dy in enumerate((2, 1, 3)):
-        send(rows.at[core, :, y], rows.at[core, :, y], s_act.at[1], r_act2, at_y(dy))
+    for k in range(2):
+        drain(rows.at[core, 0, pl.ds(0, 4)], r_act1.at[k])
+        block = rows.at[core, y, pl.ds(4 * k, 4)]
+        for dy in (2, 1, 3):
+            send(block, block, s_act.at[1], r_act2, at_y(dy))
 
     @pl.when(sec > 0)
     def _():
@@ -233,15 +236,15 @@
         for yy in range(NY):
             weights[zz, yy, :, 128:256] = dot(gain_of(zz * NY + yy), wq_sib[zz, yy]).astype(BF16)
 
-    drain(rows.at[core, :, pl.ds(0, 3)], r_act2)
+    drain(rows.at[core, pl.ds(0, 3)], r_act2)
     send(rows.at[core], rows.at[core], s_act.at[2], r_act3, sibling)
     drain(rows.at[core], r_act3)
 
     for p in range(2):
-        for zz in range(NZ):
-            for yy in range(NY):
-                at = ((p * NZ + zz) * NY + yy) * 40
-                rowsf[at : at + 40, :] = rows[p, zz, yy].astype(F32)
+        for yy in range(NY):
+            for zz in range(NZ):
+                at = ((p * NY + yy) * NZ + zz) * 40
+                rowsf[at : at + 40, :] = rows[p, yy, zz].astype(F32)
     load_mw.wait()
     acc = jnp.broadcast_to(bias_ref[...].astype(F32), (64, 128))
     for k in range(20):
@@ -281,7 +284,8 @@
         offset = pos - begin
         is_image = (offset >= 1) & (offset <= count)
         row = earlier + offset - 1 - m * 128
-        slot = (row & 64) + ((row & 1) << 5) + ((row & 63) >> 1)
+        away = (z + NZ + 1 - ((row & 63) >> 3)) & (NZ - 1)
+        slot = (row & 64) + ((row & 1) << 5) + (((row >> 1) & 3) << 3) + away
         chosen = (iota((count_here, 128), 1) == slot) & is_image
         picked = dot(
             jnp.where(chosen, 1.0, 0.0).astype(BF16), merged[2 * m : 2 * m + 2].reshape(128, 128)
@@ -527,8 +531,8 @@
             values[here, :] = kv[:, 128:256]
             attend(t)
 
-    drain(rows.at[core, pl.ds(0, 7), 0], s_act.at[0])
-    drain(rows.at[core, :, pl.ds(0, 3)], s_act.at[1])
+    drain(rows.at[core, 0, pl.ds(0, 7)], s_act.at[0])
+    drain(rows.at[core, pl.ds(0, 3)], s_act.at[1])
     drain(rows.at[core], s_act.at[2])
     drain(wq_sib, s_wq)
     drain(kvrx.at[pl.ds(0, 7)], s_kv)
@@ -568,7 +572,7 @@
         pltpu.VMEM((64, 128), F32),
         pltpu.VMEM((40, 128), F32),
         pltpu.VMEM((40, 128), BF16),
-        pltpu.VMEM((2, NZ, NY, 40, 128), BF16),
+        pltpu.VMEM((2, NY, NZ, 40, 128), BF16),
         pltpu.VMEM((2560, 128), F32),
         pltpu.VMEM((64, 128), BF16),
         pltpu.VMEM((4, 64, 128), BF16),
@@ -593,7 +597,7 @@
         dma,
         dma,
         dma((3,)),
-        dma,
+        dma((2,)),
         dma,
         dma,
         dma,

time: 120 us -> 120 us (level)
  no operation moved by 1% of the time
where the time goes in v5:
time: 120 us; the launch traced here: 119 us
  Pallas kernels  117 us (98%)
  local copies, waits for them, and re-layouts  1.53 us (1%)
    pallas_call x1, Pallas kernels, shards(): pl.pallas_call(kernel, out_shape=jax.ShapeDtypeStruct((tokens, 128), BF16...  117 us

profile of v5, /device:TPU:39, one launch (start us, length us, event | category | flops | bytes accessed | tf_op | source)
XLA Modules:
  0.0 119.0 jit_solution(15741324663720497287)
XLA Ops:
  0.0 117.5 %prefill.1 = bf16[320,128]{1,0:T(8,128)(2,1)} custom-call(s32[2,4]{1,0:T(2,128)} %images_ref.1, s32[2,4]{1,0:T(2,128)} %texts_ref.1, bf16[320,128]{1,0:T(8,128)(2,1)} %text_ref.1, bf16[1,5120]{1,0:T(2,128)(2,1)} %patch_ref.1, bf16[5120,128]{1,0:T(8,128)(2,1)} %mw_ref.1, bf16[1,128]{1,0:T(2,128)(2,1)} %bitcast.13, bf16[1,8192]{1,0:T(2,128)(2,1)} %gain_ref.1, ...), custom_call_target="tpu_custom_call" | custom-call | tf_op jit(solution)/shard_map/prefill/pallas_call | solution.py:624
  117.5 1.5 %copy.12 = bf16[1,320,128]{2,1,0:T(8,128)(2,1)} copy(bf16[1,320,128]{2,1,0:T(8,128)(2,1)} %bitcast.10) | data formatting | bytes 163840

commit v6 on v5

--- a/solution.py
+++ b/solution.py
@@ -436,9 +436,9 @@
             return step
 
         sums = jnp.zeros((tc, 512), F32), jnp.zeros((tc, 128), F32)
-        sums = lax.fori_loop(0, NZ, products(y, (y + 1) % NY), sums, unroll=4)
+        sums = lax.fori_loop(0, NZ, products(y, (y + 1) % NY), sums, unroll=8)
         drain(states.at[t, 0], r_far.at[t])
-        acc, squares = lax.fori_loop(0, NZ, products((y + 2) % NY, (y + 3) % NY), sums, unroll=4)
+        acc, squares = lax.fori_loop(0, NZ, products((y + 2) % NY, (y + 3) % NY), sums, unroll=8)
         total = jnp.broadcast_to(jnp.sum(squares, axis=1, keepdims=True), (tc, 128))
         own_q, own_kv = acc[:, 0:128], acc[:, 256:512]
         xs[t, :, 0:128] = acc[:, 128:256]

time: 120 us -> 120 us (level)
  no operation moved by 1% of the time
where the time goes in v6:
time: 120 us
  Pallas kernels  118 us (98%)
  local copies, waits for them, and re-layouts  1.53 us (1%)
    pallas_call x1, Pallas kernels, shards(): pl.pallas_call(kernel, out_shape=jax.ShapeDtypeStruct((tokens, 128), BF16...  118 us

profile of v6, /device:TPU:39, one launch (start us, length us, event | category | flops | bytes accessed | tf_op | source)
XLA Modules:
  0.0 119.5 jit_solution(14914238632079845342)
XLA Ops:
  0.0 118.0 %prefill.1 = bf16[320,128]{1,0:T(8,128)(2,1)} custom-call(s32[2,4]{1,0:T(2,128)} %images_ref.1, s32[2,4]{1,0:T(2,128)} %texts_ref.1, bf16[320,128]{1,0:T(8,128)(2,1)} %text_ref.1, bf16[1,5120]{1,0:T(2,128)(2,1)} %patch_ref.1, bf16[5120,128]{1,0:T(8,128)(2,1)} %mw_ref.1, bf16[1,128]{1,0:T(2,128)(2,1)} %bitcast.13, bf16[1,8192]{1,0:T(2,128)(2,1)} %gain_ref.1, ...), custom_call_target="tpu_custom_call" | custom-call | tf_op jit(solution)/shard_map/prefill/pallas_call | solution.py:624
  118.0 1.5 %copy.12 = bf16[1,320,128]{2,1,0:T(8,128)(2,1)} copy(bf16[1,320,128]{2,1,0:T(8,128)(2,1)} %bitcast.10) | data formatting | bytes 163840
